TPU v7x, 1024 devices: a whole 4x4x32 slice. The times are simulated.
1024 devices in a mesh: lat: 64 (over x, y, z_hi), lon: 16 (over z_lo, core).
Axes of the slice: x: 4, y: 4, z: 32 (z_hi: 4, z_lo: 8; z = z_hi * 8 + z_lo), core: 2. Of those that a mesh axis runs over, the one named last changes fastest.
Arguments:
- query_field: bfloat16 [512, 256, 512], P('lat', 'lon'), may hold values from -6 to 6
- key_field: bfloat16 [512, 256, 512], P('lat', 'lon'), may hold values from -6 to 6
- value_field: bfloat16 [512, 256, 512], P('lat', 'lon'), may hold values from -6 to 6
- out_grad: bfloat16 [512, 256, 512], P('lat', 'lon'), may hold values from -24 to 24
- pole_reach: int32 [2, 256], replicated, may hold values from 0 to 6
Outputs:
- query_grad: bfloat16 [512, 256, 512], P('lat', 'lon')
- key_grad: bfloat16 [512, 256, 512], P('lat', 'lon')
- value_grad: bfloat16 [512, 256, 512], P('lat', 'lon')
All inputs are finite; a program needn't handle non-finite values.
Results may differ from a plain program's by a relative error of at most 0.012.
The roundings to bfloat16 on the way count: a program that leaves them out, or rounds other values in their place, can miss the bound.
Values may be sent and summed in bfloat16 or wider, within the bound.
A program may use at most 32 MiB of HBM per device.

v0:
```python
import math

import jax
import jax.numpy as jnp
from jax import lax
from jax.sharding import PartitionSpec as P

HEAD_DIM = 32
RADIUS = 6


def with_halo(block, sides, width):
    for axis, dim in sides:
        count = lax.axis_size(axis)
        forward = [(i, i + 1) for i in range(count - 1)]
        forward.append((count - 1, 0))
        backward = [(target, source) for source, target in forward]
        low = lax.ppermute(
            lax.slice_in_dim(block, block.shape[dim] - width, None, axis=dim), axis, forward
        )
        high = lax.ppermute(lax.slice_in_dim(block, 0, width, axis=dim), axis, backward)
        block = jnp.concatenate([low, block, high], axis=dim)
    return block


def for_sending(array):

    def short(part):
        return part.astype(jnp.bfloat16) if part.dtype == jnp.float32 else part

    return jax.tree.map(short, array)


def swapped(block, axis, apart):
    count = lax.axis_size(axis)
    route = []
    for low in range(count):
        high = low | 1 << apart
        if high != low and high < count:
            route += [(low, high), (high, low)]
    return lax.ppermute(block, axis, route)


def lookup_row(table_row, positions, extent):
    match = positions[:, None] == jnp.arange(extent, dtype=jnp.int32)[None, :]
    return jnp.sum(jnp.where(match, table_row[None, :], 0), axis=1)


def neighbour_mask(
    pole_reach, lat_index, lon_index, block_rows, block_cols, total_rows, total_cols
):
    local_rows = jnp.arange(block_rows, dtype=jnp.int32)
    local_cols = jnp.arange(block_cols, dtype=jnp.int32)
    outer_rows = jnp.arange(block_rows + 2 * RADIUS, dtype=jnp.int32)
    outer_cols = jnp.arange(block_cols + 2 * RADIUS, dtype=jnp.int32)
    global_rows = lat_index * block_rows + local_rows
    global_cols = lon_index * block_cols + local_cols
    padded_rows = lat_index * block_rows + outer_rows
    key_cols = jnp.remainder(
        lon_index * block_cols + outer_cols - RADIUS + total_cols // 2, total_cols
    )
    north_band = padded_rows < RADIUS
    south_band = padded_rows >= total_rows + RADIUS
    north_depth = RADIUS - 1 - padded_rows
    south_depth = padded_rows - total_rows - RADIUS
    north_key = lookup_row(pole_reach[0], key_cols, total_cols)
    south_key = lookup_row(pole_reach[1], key_cols, total_cols)
    key_valid = jnp.where(
        north_band[:, None],
        north_key[None, :] > north_depth[:, None],
        jnp.where(south_band[:, None], south_key[None, :] > south_depth[:, None], True),
    )
    north_query = lookup_row(pole_reach[0], global_cols, total_cols)[None, :] > global_rows[:, None]
    south_query = (
        lookup_row(pole_reach[1], global_cols, total_cols)[None, :]
        > (total_rows - 1 - global_rows)[:, None]
    )
    row_near = (outer_rows[None, :] >= local_rows[:, None]) & (
        outer_rows[None, :] <= local_rows[:, None] + 2 * RADIUS
    )
    col_near = (outer_cols[None, :] >= local_cols[:, None]) & (
        outer_cols[None, :] <= local_cols[:, None] + 2 * RADIUS
    )
    allowed = row_near[:, None, :, None] & col_near[None, :, None, :] & key_valid[None, None, :, :]
    allowed = allowed & (
        jnp.logical_not(north_band)[None, None, :, None] | north_query[:, :, None, None]
    )
    allowed = allowed & (
        jnp.logical_not(south_band)[None, None, :, None] | south_query[:, :, None, None]
    )
    return allowed.reshape(block_rows * block_cols, -1)


def polar_slab(padded, block_rows):
    return jnp.concatenate(
        [padded[RADIUS : 2 * RADIUS], padded[block_rows : block_rows + RADIUS]], axis=0
    )


def splice(padded, north_part, south_part, block_rows, is_north, is_south):
    northern = jnp.concatenate([jnp.flip(north_part, axis=0), padded[RADIUS:]], axis=0)
    padded = jnp.where(is_north, northern, padded)
    southern = jnp.concatenate(
        [padded[: block_rows + RADIUS], jnp.flip(south_part, axis=0)], axis=0
    )
    return jnp.where(is_south, southern, padded)


def heads_last_cells(field, group_count, group_size):
    cell_count = field.shape[0]
    return field.reshape(cell_count, group_count, group_size, HEAD_DIM).transpose(1, 2, 3, 0)


def cells_first(stacked, cell_count):
    return stacked.reshape(-1, cell_count).T


def query_block(query_rows, key_rows, value_rows, grad_rows, allowed, head_count):
    scale = 1.0 / math.sqrt(HEAD_DIM)
    group_size = math.gcd(head_count, 4)
    group_count = head_count // group_size

    def query_one_group(pieces):
        query_part, key_part, value_part, grad_part = pieces
        scores = (
            jnp.einsum("hdq,hdk->hqk", query_part, key_part, preferred_element_type=jnp.float32)
            * scale
        )
        masked = jnp.where(allowed[None], scores, -1e30)
        row_max = jnp.max(masked, axis=2, keepdims=True)
        row_total = jnp.sum(
            jnp.where(allowed[None], jnp.exp(masked - row_max), 0.0), axis=2, keepdims=True
        )
        log_total = row_max + jnp.log(row_total)
        probs = jnp.where(allowed[None], jnp.exp(scores - log_total), 0.0)
        probs_half = probs.astype(jnp.bfloat16)
        attended = jnp.einsum(
            "hqk,hdk->hdq", probs_half, value_part, preferred_element_type=jnp.float32
        )
        grad_dot = jnp.sum(grad_part.astype(jnp.float32) * attended, axis=1)
        grad_probs = jnp.einsum(
            "hdq,hdk->hqk", grad_part, value_part, preferred_element_type=jnp.float32
        )
        grad_scores = (probs * (grad_probs - grad_dot[:, :, None])).astype(jnp.bfloat16)
        query_grad = (
            jnp.einsum("hqk,hdk->hdq", grad_scores, key_part, preferred_element_type=jnp.float32)
            * scale
        )
        return (log_total[:, :, 0], grad_dot, query_grad.astype(jnp.bfloat16))

    log_groups, dot_groups, grad_groups = lax.map(
        query_one_group,
        (
            heads_last_cells(query_rows, group_count, group_size),
            heads_last_cells(key_rows, group_count, group_size),
            heads_last_cells(value_rows, group_count, group_size),
            heads_last_cells(grad_rows, group_count, group_size),
        ),
    )
    token_count = query_rows.shape[0]
    return (
        cells_first(log_groups, token_count),
        cells_first(dot_groups, token_count),
        cells_first(grad_groups, token_count),
    )


def key_block(
    key_rows, value_rows, query_outer, grad_outer, log_outer, dot_outer, allowed, head_count
):
    scale = 1.0 / math.sqrt(HEAD_DIM)
    group_size = math.gcd(head_count, 4)
    group_count = head_count // group_size
    outer_count = query_outer.shape[0]
    log_groups = log_outer.reshape(outer_count, group_count, group_size).transpose(1, 2, 0)
    dot_groups = dot_outer.reshape(outer_count, group_count, group_size).transpose(1, 2, 0)

    def key_one_group(pieces):
        key_part, value_part, query_part, grad_part, log_part, dot_part = pieces
        scores = (
            jnp.einsum("hdk,hdq->hkq", key_part, query_part, preferred_element_type=jnp.float32)
            * scale
        )
        probs = jnp.where(allowed[None], jnp.exp(scores - log_part[:, None, :]), 0.0)
        probs_half = probs.astype(jnp.bfloat16)
        value_grad = jnp.einsum(
            "hkq,hdq->hdk", probs_half, grad_part, preferred_element_type=jnp.float32
        )
        grad_probs = jnp.einsum(
            "hdk,hdq->hkq", value_part, grad_part, preferred_element_type=jnp.float32
        )
        grad_scores = (probs * (grad_probs - dot_part[:, None, :])).astype(jnp.bfloat16)
        key_grad = (
            jnp.einsum("hkq,hdq->hdk", grad_scores, query_part, preferred_element_type=jnp.float32)
            * scale
        )
        return (key_grad.astype(jnp.bfloat16), value_grad.astype(jnp.bfloat16))

    key_groups, value_groups = lax.map(
        key_one_group,
        (
            heads_last_cells(key_rows, group_count, group_size),
            heads_last_cells(value_rows, group_count, group_size),
            heads_last_cells(query_outer, group_count, group_size),
            heads_last_cells(grad_outer, group_count, group_size),
            log_groups,
            dot_groups,
        ),
    )
    token_count = key_rows.shape[0]
    return (cells_first(key_groups, token_count), cells_first(value_groups, token_count))


def flatten_cells(field):
    return field.reshape(-1, field.shape[-1])


def shards(query_field, key_field, value_field, out_grad, pole_reach):
    block_rows, block_cols, model_width = query_field.shape
    head_count = model_width // HEAD_DIM
    lat_count = lax.axis_size("lat")
    lon_count = lax.axis_size("lon")
    lat_index = lax.axis_index("lat")
    lon_index = lax.axis_index("lon")
    pair_bit = lon_count.bit_length() - 2
    is_north = lat_index == 0
    is_south = lat_index == lat_count - 1
    allowed = neighbour_mask(
        pole_reach,
        lat_index,
        lon_index,
        block_rows,
        block_cols,
        block_rows * lat_count,
        block_cols * lon_count,
    )

    def assemble_both(padded_set, partner_set):
        return tuple(
            (
                splice(padded, partner[:RADIUS], partner[RADIUS:], block_rows, is_north, is_south)
                for padded, partner in zip(padded_set, partner_set)
            )
        )

    padded_set = (
        with_halo(query_field, (("lat", 0), ("lon", 1)), RADIUS),
        with_halo(key_field, (("lat", 0), ("lon", 1)), RADIUS),
        with_halo(value_field, (("lat", 0), ("lon", 1)), RADIUS),
        with_halo(out_grad, (("lat", 0), ("lon", 1)), RADIUS),
    )
    partner_set = swapped(
        for_sending(tuple((polar_slab(padded, block_rows) for padded in padded_set))),
        "lon",
        pair_bit,
    )
    query_outer, key_outer, value_outer, grad_outer = assemble_both(padded_set, partner_set)
    log_total, grad_dot, query_grad = query_block(
        flatten_cells(query_field),
        flatten_cells(key_outer),
        flatten_cells(value_outer),
        flatten_cells(out_grad),
        allowed,
        head_count,
    )
    stats = (
        log_total.reshape(block_rows, block_cols, head_count),
        grad_dot.reshape(block_rows, block_cols, head_count),
    )
    stat_padded = (
        with_halo(stats[0], (("lat", 0), ("lon", 1)), RADIUS),
        with_halo(stats[1], (("lat", 0), ("lon", 1)), RADIUS),
    )
    stat_partner = swapped(
        tuple((polar_slab(padded, block_rows) for padded in stat_padded)), "lon", pair_bit
    )
    log_outer, dot_outer = assemble_both(stat_padded, stat_partner)
    key_grad, value_grad = key_block(
        flatten_cells(key_field),
        flatten_cells(value_field),
        flatten_cells(query_outer),
        flatten_cells(grad_outer),
        flatten_cells(log_outer),
        flatten_cells(dot_outer),
        allowed,
        head_count,
    )
    grid_shape = (block_rows, block_cols, model_width)
    return (
        query_grad.reshape(grid_shape),
        key_grad.reshape(grid_shape),
        value_grad.reshape(grid_shape),
    )


def solution(mesh):
    placed = (
        P("lat", "lon", None),
        P("lat", "lon", None),
        P("lat", "lon", None),
        P("lat", "lon", None),
        P(),
    )
    return jax.shard_map(
        shards,
        mesh=mesh,
        in_specs=placed,
        out_specs=(P("lat", "lon", None), P("lat", "lon", None), P("lat", "lon", None)),
        check_vma=False,
    )
```

profile of v0, /device:TPU:1, one launch (start us, length us, event | category | flops | bytes accessed | tf_op | source)
XLA Modules:
  0.0 424.3 jit_solution(14410506412322874282)
XLA Ops:
  0.7 1.7 fusion.106
  2.3 16.3 %collective-permute-start.5 = (bf16[6,16,512]{2,1,0:T(8,128)(2,1)}, bf16[6,16,512]{2,1,0:T(8,128)(2,1)S(1)}, u32[]{:S(2)}, u32[]{:S(2)}) collective-permute-start(bf16[6,16,512]{2,1,0:T(8,128)(2,1)} %get-tuple-element.337), channel_id=1, source_target_pairs={{0,16},{16,32},{32,48},{48,64},{64,80},{80,96},{96,112},{112,128},... | collective-permute-start | bytes 294920 | tf_op jit(solution)/shard_map/ppermute | solution.py:18
  18.6 14.0 %collective-permute-start.6 = (bf16[6,16,512]{2,1,0:T(8,128)(2,1)}, bf16[6,16,512]{2,1,0:T(8,128)(2,1)S(1)}, u32[]{:S(2)}, u32[]{:S(2)}) collective-permute-start(bf16[6,16,512]{2,1,0:T(8,128)(2,1)} %get-tuple-element.336), channel_id=1, source_target_pairs={{16,0},{32,16},{48,32},{64,48},{80,64},{96,80},{112,96},{128,112},... | collective-permute-start | bytes 294920 | tf_op jit(solution)/shard_map/ppermute | solution.py:21
  33.6 3.5 collective-permute-start
  37.1 14.7 %collective-permute-start.1 = (bf16[6,16,512]{2,1,0:T(8,128)(2,1)S(1)}, bf16[6,16,512]{2,1,0:T(8,128)(2,1)S(1)}, u32[]{:S(2)}, u32[]{:S(2)}) collective-permute-start(bf16[6,16,512]{2,1,0:T(8,128)(2,1)S(1)} %get-tuple-element.338), channel_id=1, source_target_pairs={{16,0},{32,16},{48,32},{64,48},{80,64},{96,80},{112,96},{128,112},... | collective-permute-start | bytes 294920 | tf_op jit(solution)/shard_map/ppermute | solution.py:21
  51.8 1.6 fusion.105
  53.4 2.0 collective-permute-start.10
  63.5 16.3 %collective-permute-start.11 = (bf16[6,16,512]{2,1,0:T(8,128)(2,1)}, bf16[6,16,512]{2,1,0:T(8,128)(2,1)S(1)}, u32[]{:S(2)}, u32[]{:S(2)}) collective-permute-start(bf16[6,16,512]{2,1,0:T(8,128)(2,1)} %get-tuple-element.334), channel_id=1, source_target_pairs={{16,0},{32,16},{48,32},{64,48},{80,64},{96,80},{112,96},{128,112},... | collective-permute-start | bytes 294920 | tf_op jit(solution)/shard_map/ppermute | solution.py:21
  79.9 1.9 collective-permute-start.20
  81.9 16.3 %collective-permute-start.21 = (bf16[6,16,512]{2,1,0:T(8,128)(2,1)S(1)}, bf16[6,16,512]{2,1,0:T(8,128)(2,1)S(1)}, u32[]{:S(2)}, u32[]{:S(2)}) collective-permute-start(bf16[6,16,512]{2,1,0:T(8,128)(2,1)S(1)} %copy-done.29), channel_id=1, source_target_pairs={{16,0},{32,16},{48,32},{64,48},{80,64},{96,80},{112,96},{128,112},... | collective-permute-start | bytes 294920 | tf_op jit(solution)/shard_map/ppermute | solution.py:21
  98.3 5.2 %collective-permute-start.7 = (bf16[20,6,512]{2,1,0:T(8,128)(2,1)S(1)}, bf16[20,6,512]{2,1,0:T(8,128)(2,1)S(1)}, u32[]{:S(2)}, u32[]{:S(2)}) collective-permute-start(bf16[20,6,512]{2,1,0:T(8,128)(2,1)S(1)} %get-tuple-element.316), channel_id=1, source_target_pairs={{0,1},{1,2},{2,3},{3,4},{4,5},{5,6},{6,7},{7,8},{8,9},{9,10},{10,1... | collective-permute-start | bytes 368648 | tf_op jit(solution)/shard_map/ppermute | solution.py:18
  104.2 3.1 collective-permute-start.8
  108.2 2.4 collective-permute-start.2
  110.7 9.8 %collective-permute-start.3 = (bf16[20,6,512]{2,1,0:T(8,128)(2,1)S(1)}, bf16[20,6,512]{2,1,0:T(8,128)(2,1)S(1)}, u32[]{:S(2)}, u32[]{:S(2)}) collective-permute-start(bf16[20,6,512]{2,1,0:T(8,128)(2,1)S(1)} %get-tuple-element.319), channel_id=1, source_target_pairs={{1,0},{2,1},{3,2},{4,3},{5,4},{6,5},{7,6},{8,7},{9,8},{10,9},{11,1... | collective-permute-start | bytes 368648 | tf_op jit(solution)/shard_map/ppermute | solution.py:21
  120.5 1.9 collective-permute-start.12
  122.6 10.2 %collective-permute-start.13 = (bf16[20,6,512]{2,1,0:T(8,128)(2,1)S(1)}, bf16[20,6,512]{2,1,0:T(8,128)(2,1)S(1)}, u32[]{:S(2)}, u32[]{:S(2)}) collective-permute-start(bf16[20,6,512]{2,1,0:T(8,128)(2,1)S(1)} %get-tuple-element.315), channel_id=1, source_target_pairs={{1,0},{2,1},{3,2},{4,3},{5,4},{6,5},{7,6},{8,7},{9,8},{10,9},{11,1... | collective-permute-start | bytes 368648 | tf_op jit(solution)/shard_map/ppermute | solution.py:21
  132.8 1.9 collective-permute-start.22
  135.2 10.2 %collective-permute-start.23 = (bf16[20,6,512]{2,1,0:T(8,128)(2,1)S(1)}, bf16[20,6,512]{2,1,0:T(8,128)(2,1)S(1)}, u32[]{:S(2)}, u32[]{:S(2)}) collective-permute-start(bf16[20,6,512]{2,1,0:T(8,128)(2,1)S(1)} %get-tuple-element.313), channel_id=1, source_target_pairs={{1,0},{2,1},{3,2},{4,3},{5,4},{6,5},{7,6},{8,7},{9,8},{10,9},{11,1... | collective-permute-start | bytes 368648 | tf_op jit(solution)/shard_map/ppermute | solution.py:21
  147.1 1.9 collective-permute-start.9
  149.1 7.3 %collective-permute-start.4 = (bf16[12,28,512]{2,1,0:T(8,128)(2,1)S(1)}, bf16[12,28,512]{2,1,0:T(8,128)(2,1)S(1)}, u32[]{:S(2)}, u32[]{:S(2)}) collective-permute-start(bf16[12,28,512]{2,1,0:T(8,128)(2,1)S(1)} %pad_maximum_fusion.4), channel_id=1, source_target_pairs={{0,8},{8,0},{1,9},{9,1},{2,10},{10,2},{3,11},{11,3},{4,12},{12,4},... | collective-permute-start | bytes 1032200 | tf_op jit(solution)/shard_map/ppermute | solution.py:41
  157.1 1.9 collective-permute-start.14
  161.1 7.6 %collective-permute-start.24 = (bf16[12,28,512]{2,1,0:T(8,128)(2,1)}, bf16[12,28,512]{2,1,0:T(8,128)(2,1)}, u32[]{:S(2)}, u32[]{:S(2)}) collective-permute-start(bf16[12,28,512]{2,1,0:T(8,128)(2,1)} %pad_maximum_fusion.7), channel_id=1, source_target_pairs={{0,8},{8,0},{1,9},{9,1},{2,10},{10,2},{3,11},{11,3},{4,12},{12,4},... | collective-permute-start | bytes 1032200 | tf_op jit(solution)/shard_map/ppermute | solution.py:41
  168.7 84.3 %collective-permute-done.9 = bf16[12,28,512]{2,1,0:T(8,128)(2,1)S(1)} collective-permute-done((bf16[12,28,512]{2,1,0:T(8,128)(2,1)S(1)}, bf16[12,28,512]{2,1,0:T(8,128)(2,1)S(1)}, u32[]{:S(2)}, u32[]{:S(2)}) %collective-permute-start.9) | collective-permute-done | bytes 344096 | tf_op jit(solution)/shard_map/ppermute | solution.py:41
  253.7 7.7 %collective-permute-done.4 = bf16[12,28,512]{2,1,0:T(8,128)(2,1)S(1)} collective-permute-done((bf16[12,28,512]{2,1,0:T(8,128)(2,1)S(1)}, bf16[12,28,512]{2,1,0:T(8,128)(2,1)S(1)}, u32[]{:S(2)}, u32[]{:S(2)}) %collective-permute-start.4) | collective-permute-done | bytes 344096 | tf_op jit(solution)/shard_map/ppermute | solution.py:41
  262.8 2.1 maximum_select_fusion
  266.8 3.6 select_n.164
  270.4 2.8 copy.37
  274.2 3.6 select_n.161
  277.9 2.1 copy.35
  280.0 17.7 %while.28 = (s32[]{:T(128)}, f32[4,4,128]{2,1,0:T(4,128)S(1)}, f32[4,4,128]{2,1,0:T(4,128)S(1)}, bf16[4,4,32,128]{3,2,1,0:T(8,128)(2,1)S(1)}, bf16[4,4,32,128]{3...) while((s32[]{:T(128)}, f32[4,4,128]{2,1,0:T(4,128)S(1)}, ...), condition=%wide.region_8.9_spmd.clone, body=%wide.region_4.8_spmd.clone.sunk | while | flops 78068736 | bytes 8350009 | solution.py:151
  299.2 1.9 collective-permute-start.25
  301.8 16.3 %collective-permute-start.26 = (f32[6,16,16]{1,0,2:T(8,128)}, f32[6,16,16]{1,0,2:T(8,128)}, u32[]{:S(2)}, u32[]{:S(2)}) collective-permute-start(f32[6,16,16]{1,0,2:T(8,128)} %slice.257), channel_id=1, source_target_pairs={{16,0},{32,16},{48,32},{64,48},{80,64},{96,80},{112,96},{128,112},... | collective-permute-start | bytes 18440 | tf_op jit(solution)/shard_map/ppermute | solution.py:21
  321.1 2.8 maximum_select_fusion.4
  324.9 3.6 select_n.175
  328.5 2.1 copy.42
  331.3 1.9 collective-permute-start.15
  334.0 16.5 %collective-permute-start.16 = (f32[6,16,16]{1,0,2:T(8,128)}, f32[6,16,16]{1,0,2:T(8,128)}, u32[]{:S(2)}, u32[]{:S(2)}) collective-permute-start(f32[6,16,16]{1,0,2:T(8,128)} %slice.235), channel_id=1, source_target_pairs={{16,0},{32,16},{48,32},{64,48},{80,64},{96,80},{112,96},{128,112},... | collective-permute-start | bytes 18440 | tf_op jit(solution)/shard_map/ppermute | solution.py:21
  352.5 3.6 select_n.167
  356.2 2.9 copy.39
  360.9 1.9 collective-permute-start.27
  362.8 3.6 collective-permute-start.28
  367.4 1.9 collective-permute-start.17
  369.4 10.2 %collective-permute-start.18 = (f32[20,6,16]{1,0,2:T(8,128)S(1)}, f32[20,6,16]{1,0,2:T(8,128)S(1)}, u32[]{:S(2)}, u32[]{:S(2)}) collective-permute-start(f32[20,6,16]{1,0,2:T(8,128)S(1)} %get-tuple-element.327), channel_id=1, source_target_pairs={{1,0},{2,1},{3,2},{4,3},{5,4},{6,5},{7,6},{8,7},{9,8},{10,9},{11,1... | collective-permute-start | bytes 23048 | tf_op jit(solution)/shard_map/ppermute | solution.py:21
  380.8 1.9 collective-permute-start.29
  383.9 7.3 %collective-permute-start.19 = (f32[12,28,16]{1,0,2:T(8,128)S(1)}, f32[12,28,16]{1,0,2:T(8,128)S(1)}, u32[]{:S(2)}, u32[]{:S(2)}) collective-permute-start(f32[12,28,16]{1,0,2:T(8,128)S(1)} %pad_maximum_fusion.12), channel_id=1, source_target_pairs={{0,8},{8,0},{1,9},{9,1},{2,10},{10,2},{3,11},{11,3},{4,12},{12,4},... | collective-permute-start | bytes 64520 | tf_op jit(solution)/shard_map/ppermute | solution.py:41
  391.1 9.3 %collective-permute-done.29 = f32[12,28,16]{1,0,2:T(8,128)S(1)} collective-permute-done((f32[12,28,16]{1,0,2:T(8,128)S(1)}, f32[12,28,16]{1,0,2:T(8,128)S(1)}, u32[]{:S(2)}, u32[]{:S(2)}) %collective-permute-start.29) | collective-permute-done | bytes 21536 | tf_op jit(solution)/shard_map/ppermute | solution.py:41
  400.7 2.1 collective-permute-done.19
  403.2 19.6 %while.29 = (s32[]{:T(128)}, bf16[4,4,32,128]{3,2,1,0:T(8,128)(2,1)S(1)}, bf16[4,4,32,128]{3,2,1,0:T(8,128)(2,1)S(1)}, bf16[4,4,32,560]{3,2,1,0:T(8,128)(2,1)S(1...) while((s32[]{:T(128)}, ...), condition=%wide.region_10.11_spmd.clone, body=%wide.region_9.10_spmd.clone.sunk | while | flops 75743232 | bytes 4724001 | solution.py:199
  (284 shorter events, 74.0 us)
Async XLA Ops:
  0.6 57.4 %copy-start.10 = (bf16[8,16,512]{2,1,0:T(8,128)(2,1)S(1)}, bf16[8,16,512]{2,1,0:T(8,128)(2,1)}, u32[]{:S(2)}) copy-start(bf16[8,16,512]{2,1,0:T(8,128)(2,1)} %param.9) | copy-start | bytes 393220
  0.6 56.1 %copy-start.11 = (bf16[8,16,512]{2,1,0:T(8,128)(2,1)S(1)}, bf16[8,16,512]{2,1,0:T(8,128)(2,1)}, u32[]{:S(2)}) copy-start(bf16[8,16,512]{2,1,0:T(8,128)(2,1)} %param.12) | copy-start | bytes 393220
  2.3 61.2 %collective-permute-start.5 = (bf16[6,16,512]{2,1,0:T(8,128)(2,1)}, bf16[6,16,512]{2,1,0:T(8,128)(2,1)S(1)}, u32[]{:S(2)}, u32[]{:S(2)}) collective-permute-start(bf16[6,16,512]{2,1,0:T(8,128)(2,1)} %get-tuple-element.337), channel_id=1, source_target_pairs={{0,16},{16,32},{32,48},{48,64},{64,80},{80,96},{96,112},{112,128},... | collective-permute-start | bytes 294920 | tf_op jit(solution)/shard_map/ppermute | solution.py:18
  18.6 40.0 %copy-start.9 = (bf16[8,16,512]{2,1,0:T(8,128)(2,1)S(1)}, bf16[8,16,512]{2,1,0:T(8,128)(2,1)}, u32[]{:S(2)}) copy-start(bf16[8,16,512]{2,1,0:T(8,128)(2,1)} %param.10) | copy-start | bytes 393220
  18.6 61.3 %collective-permute-start.6 = (bf16[6,16,512]{2,1,0:T(8,128)(2,1)}, bf16[6,16,512]{2,1,0:T(8,128)(2,1)S(1)}, u32[]{:S(2)}, u32[]{:S(2)}) collective-permute-start(bf16[6,16,512]{2,1,0:T(8,128)(2,1)} %get-tuple-element.336), channel_id=1, source_target_pairs={{16,0},{32,16},{48,32},{64,48},{80,64},{96,80},{112,96},{128,112},... | collective-permute-start | bytes 294920 | tf_op jit(solution)/shard_map/ppermute | solution.py:21
  33.6 48.3 %collective-permute-start = (bf16[6,16,512]{2,1,0:T(8,128)(2,1)S(1)}, bf16[6,16,512]{2,1,0:T(8,128)(2,1)S(1)}, u32[]{:S(2)}, u32[]{:S(2)}) collective-permute-start(bf16[6,16,512]{2,1,0:T(8,128)(2,1)S(1)} %get-tuple-element.339), channel_id=1, source_target_pairs={{0,16},{16,32},{32,48},{48,64},{64,80},{80,96},{96,112},{112,128},... | collective-permute-start | bytes 294920 | tf_op jit(solution)/shard_map/ppermute | solution.py:18
  37.1 61.2 %collective-permute-start.1 = (bf16[6,16,512]{2,1,0:T(8,128)(2,1)S(1)}, bf16[6,16,512]{2,1,0:T(8,128)(2,1)S(1)}, u32[]{:S(2)}, u32[]{:S(2)}) collective-permute-start(bf16[6,16,512]{2,1,0:T(8,128)(2,1)S(1)} %get-tuple-element.338), channel_id=1, source_target_pairs={{16,0},{32,16},{48,32},{64,48},{80,64},{96,80},{112,96},{128,112},... | collective-permute-start | bytes 294920 | tf_op jit(solution)/shard_map/ppermute | solution.py:21
  53.4 5.5 %copy-start.8 = (bf16[8,16,512]{2,1,0:T(8,128)(2,1)S(1)}, bf16[8,16,512]{2,1,0:T(8,128)(2,1)}, u32[]{:S(2)}) copy-start(bf16[8,16,512]{2,1,0:T(8,128)(2,1)} %param.11) | copy-start | bytes 393220
  53.4 50.1 %collective-permute-start.10 = (bf16[6,16,512]{2,1,0:T(8,128)(2,1)S(1)}, bf16[6,16,512]{2,1,0:T(8,128)(2,1)S(1)}, u32[]{:S(2)}, u32[]{:S(2)}) collective-permute-start(bf16[6,16,512]{2,1,0:T(8,128)(2,1)S(1)} %get-tuple-element.335), channel_id=1, source_target_pairs={{0,16},{16,32},{32,48},{48,64},{64,80},{80,96},{96,112},{112,128},... | collective-permute-start | bytes 294920 | tf_op jit(solution)/shard_map/ppermute | solution.py:18
  60.3 19.6 %copy-start.30 = (bf16[6,16,512]{2,1,0:T(8,128)(2,1)S(1)}, bf16[6,16,512]{2,1,0:T(8,128)(2,1)}, u32[]{:S(2)}) copy-start(bf16[6,16,512]{2,1,0:T(8,128)(2,1)} %get-tuple-element.331) | copy-start | bytes 294916
  61.4 20.5 %copy-start.29 = (bf16[6,16,512]{2,1,0:T(8,128)(2,1)S(1)}, bf16[6,16,512]{2,1,0:T(8,128)(2,1)}, u32[]{:S(2)}) copy-start(bf16[6,16,512]{2,1,0:T(8,128)(2,1)} %get-tuple-element.330) | copy-start | bytes 294916
  63.5 44.7 %collective-permute-start.11 = (bf16[6,16,512]{2,1,0:T(8,128)(2,1)}, bf16[6,16,512]{2,1,0:T(8,128)(2,1)S(1)}, u32[]{:S(2)}, u32[]{:S(2)}) collective-permute-start(bf16[6,16,512]{2,1,0:T(8,128)(2,1)} %get-tuple-element.334), channel_id=1, source_target_pairs={{16,0},{32,16},{48,32},{64,48},{80,64},{96,80},{112,96},{128,112},... | collective-permute-start | bytes 294920 | tf_op jit(solution)/shard_map/ppermute | solution.py:21
  79.9 30.8 %collective-permute-start.20 = (bf16[6,16,512]{2,1,0:T(8,128)(2,1)S(1)}, bf16[6,16,512]{2,1,0:T(8,128)(2,1)S(1)}, u32[]{:S(2)}, u32[]{:S(2)}) collective-permute-start(bf16[6,16,512]{2,1,0:T(8,128)(2,1)S(1)} %copy-done.30), channel_id=1, source_target_pairs={{0,16},{16,32},{32,48},{48,64},{64,80},{80,96},{96,112},{112,128},... | collective-permute-start | bytes 294920 | tf_op jit(solution)/shard_map/ppermute | solution.py:18
  81.9 38.6 %collective-permute-start.21 = (bf16[6,16,512]{2,1,0:T(8,128)(2,1)S(1)}, bf16[6,16,512]{2,1,0:T(8,128)(2,1)S(1)}, u32[]{:S(2)}, u32[]{:S(2)}) collective-permute-start(bf16[6,16,512]{2,1,0:T(8,128)(2,1)S(1)} %copy-done.29), channel_id=1, source_target_pairs={{16,0},{32,16},{48,32},{64,48},{80,64},{96,80},{112,96},{128,112},... | collective-permute-start | bytes 294920 | tf_op jit(solution)/shard_map/ppermute | solution.py:21
  98.3 24.3 %collective-permute-start.7 = (bf16[20,6,512]{2,1,0:T(8,128)(2,1)S(1)}, bf16[20,6,512]{2,1,0:T(8,128)(2,1)S(1)}, u32[]{:S(2)}, u32[]{:S(2)}) collective-permute-start(bf16[20,6,512]{2,1,0:T(8,128)(2,1)S(1)} %get-tuple-element.316), channel_id=1, source_target_pairs={{0,1},{1,2},{2,3},{3,4},{4,5},{5,6},{6,7},{7,8},{8,9},{9,10},{10,1... | collective-permute-start | bytes 368648 | tf_op jit(solution)/shard_map/ppermute | solution.py:18
  104.2 28.7 %collective-permute-start.8 = (bf16[20,6,512]{2,1,0:T(8,128)(2,1)S(1)}, bf16[20,6,512]{2,1,0:T(8,128)(2,1)S(1)}, u32[]{:S(2)}, u32[]{:S(2)}) collective-permute-start(bf16[20,6,512]{2,1,0:T(8,128)(2,1)S(1)} %get-tuple-element.317), channel_id=1, source_target_pairs={{1,0},{2,1},{3,2},{4,3},{5,4},{6,5},{7,6},{8,7},{9,8},{10,9},{11,1... | collective-permute-start | bytes 368648 | tf_op jit(solution)/shard_map/ppermute | solution.py:21
  108.2 26.9 %collective-permute-start.2 = (bf16[20,6,512]{2,1,0:T(8,128)(2,1)S(1)}, bf16[20,6,512]{2,1,0:T(8,128)(2,1)S(1)}, u32[]{:S(2)}, u32[]{:S(2)}) collective-permute-start(bf16[20,6,512]{2,1,0:T(8,128)(2,1)S(1)} %get-tuple-element.318), channel_id=1, source_target_pairs={{0,1},{1,2},{2,3},{3,4},{4,5},{5,6},{6,7},{7,8},{8,9},{9,10},{10,1... | collective-permute-start | bytes 368648 | tf_op jit(solution)/shard_map/ppermute | solution.py:18
  110.7 34.7 %collective-permute-start.3 = (bf16[20,6,512]{2,1,0:T(8,128)(2,1)S(1)}, bf16[20,6,512]{2,1,0:T(8,128)(2,1)S(1)}, u32[]{:S(2)}, u32[]{:S(2)}) collective-permute-start(bf16[20,6,512]{2,1,0:T(8,128)(2,1)S(1)} %get-tuple-element.319), channel_id=1, source_target_pairs={{1,0},{2,1},{3,2},{4,3},{5,4},{6,5},{7,6},{8,7},{9,8},{10,9},{11,1... | collective-permute-start | bytes 368648 | tf_op jit(solution)/shard_map/ppermute | solution.py:21
  120.5 25.6 %collective-permute-start.12 = (bf16[20,6,512]{2,1,0:T(8,128)(2,1)S(1)}, bf16[20,6,512]{2,1,0:T(8,128)(2,1)S(1)}, u32[]{:S(2)}, u32[]{:S(2)}) collective-permute-start(bf16[20,6,512]{2,1,0:T(8,128)(2,1)S(1)} %get-tuple-element.314), channel_id=1, source_target_pairs={{0,1},{1,2},{2,3},{3,4},{4,5},{5,6},{6,7},{7,8},{8,9},{9,10},{10,1... | collective-permute-start | bytes 368648 | tf_op jit(solution)/shard_map/ppermute | solution.py:18
  122.5 36.6 %copy-start.1 = (bf16[20,16,512]{2,1,0:T(8,128)(2,1)}, bf16[20,16,512]{2,1,0:T(8,128)(2,1)S(1)}, u32[]{:S(2)}) copy-start(bf16[20,16,512]{2,1,0:T(8,128)(2,1)S(1)} %constant_dynamic-update-slice_fusion.9) | copy-start | bytes 983044
  122.6 12.6 %copy-start.18 = (bf16[20,6,512]{2,1,0:T(8,128)(2,1)}, bf16[20,6,512]{2,1,0:T(8,128)(2,1)S(1)}, u32[]{:S(2)}) copy-start(bf16[20,6,512]{2,1,0:T(8,128)(2,1)S(1)} %collective-permute-done.7) | copy-start | bytes 368644
  122.6 23.6 %collective-permute-start.13 = (bf16[20,6,512]{2,1,0:T(8,128)(2,1)S(1)}, bf16[20,6,512]{2,1,0:T(8,128)(2,1)S(1)}, u32[]{:S(2)}, u32[]{:S(2)}) collective-permute-start(bf16[20,6,512]{2,1,0:T(8,128)(2,1)S(1)} %get-tuple-element.315), channel_id=1, source_target_pairs={{1,0},{2,1},{3,2},{4,3},{5,4},{6,5},{7,6},{8,7},{9,8},{10,9},{11,1... | collective-permute-start | bytes 368648 | tf_op jit(solution)/shard_map/ppermute | solution.py:21
  132.8 26.2 %collective-permute-start.22 = (bf16[20,6,512]{2,1,0:T(8,128)(2,1)S(1)}, bf16[20,6,512]{2,1,0:T(8,128)(2,1)S(1)}, u32[]{:S(2)}, u32[]{:S(2)}) collective-permute-start(bf16[20,6,512]{2,1,0:T(8,128)(2,1)S(1)} %get-tuple-element.312), channel_id=1, source_target_pairs={{0,1},{1,2},{2,3},{3,4},{4,5},{5,6},{6,7},{7,8},{8,9},{9,10},{10,1... | collective-permute-start | bytes 368648 | tf_op jit(solution)/shard_map/ppermute | solution.py:18
  135.1 10.7 %copy-start.3 = (bf16[20,28,512]{2,1,0:T(8,128)(2,1)}, bf16[20,28,512]{2,1,0:T(8,128)(2,1)S(1)}, u32[]{:S(2)}) copy-start(bf16[20,28,512]{2,1,0:T(8,128)(2,1)S(1)} %pad_maximum_fusion.1) | copy-start | bytes 1720324
  135.1 10.6 %copy-start.20 = (bf16[20,6,512]{2,1,0:T(8,128)(2,1)}, bf16[20,6,512]{2,1,0:T(8,128)(2,1)S(1)}, u32[]{:S(2)}) copy-start(bf16[20,6,512]{2,1,0:T(8,128)(2,1)S(1)} %collective-permute-done.2) | copy-start | bytes 368644
  135.2 23.9 %collective-permute-start.23 = (bf16[20,6,512]{2,1,0:T(8,128)(2,1)S(1)}, bf16[20,6,512]{2,1,0:T(8,128)(2,1)S(1)}, u32[]{:S(2)}, u32[]{:S(2)}) collective-permute-start(bf16[20,6,512]{2,1,0:T(8,128)(2,1)S(1)} %get-tuple-element.313), channel_id=1, source_target_pairs={{1,0},{2,1},{3,2},{4,3},{5,4},{6,5},{7,6},{8,7},{9,8},{10,9},{11,1... | collective-permute-start | bytes 368648 | tf_op jit(solution)/shard_map/ppermute | solution.py:21
  147.1 105.8 %collective-permute-start.9 = (bf16[12,28,512]{2,1,0:T(8,128)(2,1)S(1)}, bf16[12,28,512]{2,1,0:T(8,128)(2,1)S(1)}, u32[]{:S(2)}, u32[]{:S(2)}) collective-permute-start(bf16[12,28,512]{2,1,0:T(8,128)(2,1)S(1)} %pad_maximum_fusion.5), channel_id=1, source_target_pairs={{0,8},{8,0},{1,9},{9,1},{2,10},{10,2},{3,11},{11,3},{4,12},{12,4},... | collective-permute-start | bytes 1032200 | tf_op jit(solution)/shard_map/ppermute | solution.py:41
  149.1 112.3 %collective-permute-start.4 = (bf16[12,28,512]{2,1,0:T(8,128)(2,1)S(1)}, bf16[12,28,512]{2,1,0:T(8,128)(2,1)S(1)}, u32[]{:S(2)}, u32[]{:S(2)}) collective-permute-start(bf16[12,28,512]{2,1,0:T(8,128)(2,1)S(1)} %pad_maximum_fusion.4), channel_id=1, source_target_pairs={{0,8},{8,0},{1,9},{9,1},{2,10},{10,2},{3,11},{11,3},{4,12},{12,4},... | collective-permute-start | bytes 1032200 | tf_op jit(solution)/shard_map/ppermute | solution.py:41
  157.1 161.0 %collective-permute-start.14 = (bf16[12,28,512]{2,1,0:T(8,128)(2,1)}, bf16[12,28,512]{2,1,0:T(8,128)(2,1)}, u32[]{:S(2)}, u32[]{:S(2)}) collective-permute-start(bf16[12,28,512]{2,1,0:T(8,128)(2,1)} %pad_maximum_fusion.6), channel_id=1, source_target_pairs={{0,8},{8,0},{1,9},{9,1},{2,10},{10,2},{3,11},{11,3},{4,12},{12,4},... | collective-permute-start | bytes 1032200 | tf_op jit(solution)/shard_map/ppermute | solution.py:41
  161.1 101.7 %slice-start = ((bf16[20,28,512]{2,1,0:T(8,128)(2,1)}), bf16[14,28,512]{2,1,0:T(8,128)(2,1)S(1)}, s32[]{:S(2)}) async-start(bf16[20,28,512]{2,1,0:T(8,128)(2,1)} %copy-done.3), calls=%async_computation | async-start | bytes 917504 | tf_op jit(solution)/shard_map/slice | solution.py:101
  161.1 101.7 %slice-start.1 = ((bf16[20,28,512]{2,1,0:T(8,128)(2,1)}), bf16[14,28,512]{2,1,0:T(8,128)(2,1)S(1)}, s32[]{:S(2)}) async-start(bf16[20,28,512]{2,1,0:T(8,128)(2,1)} %copy-done.4), calls=%async_computation.1 | async-start | bytes 917504 | tf_op jit(solution)/shard_map/slice | solution.py:101
  161.1 158.9 %collective-permute-start.24 = (bf16[12,28,512]{2,1,0:T(8,128)(2,1)}, bf16[12,28,512]{2,1,0:T(8,128)(2,1)}, u32[]{:S(2)}, u32[]{:S(2)}) collective-permute-start(bf16[12,28,512]{2,1,0:T(8,128)(2,1)} %pad_maximum_fusion.7), channel_id=1, source_target_pairs={{0,8},{8,0},{1,9},{9,1},{2,10},{10,2},{3,11},{11,3},{4,12},{12,4},... | collective-permute-start | bytes 1032200 | tf_op jit(solution)/shard_map/ppermute | solution.py:41
  298.5 22.6 %copy-start.2 = (bf16[20,16,512]{2,1,0:T(8,128)(2,1)S(1)}, bf16[20,16,512]{2,1,0:T(8,128)(2,1)}, u32[]{:S(2)}) copy-start(bf16[20,16,512]{2,1,0:T(8,128)(2,1)} %copy-done.1) | copy-start | bytes 983044
  298.5 22.6 %slice-start.2 = ((bf16[20,28,512]{2,1,0:T(8,128)(2,1)}), bf16[14,28,512]{2,1,0:T(8,128)(2,1)S(1)}, s32[]{:S(2)}) async-start(bf16[20,28,512]{2,1,0:T(8,128)(2,1)} %copy-done.5), calls=%async_computation.2 | async-start | bytes 917504 | tf_op jit(solution)/shard_map/slice | solution.py:101
  298.5 22.6 %slice-start.3 = ((bf16[20,28,512]{2,1,0:T(8,128)(2,1)}), bf16[14,28,512]{2,1,0:T(8,128)(2,1)S(1)}, s32[]{:S(2)}) async-start(bf16[20,28,512]{2,1,0:T(8,128)(2,1)} %copy-done.6), calls=%async_computation.3 | async-start | bytes 917504 | tf_op jit(solution)/shard_map/slice | solution.py:101
  298.5 22.6 %copy-start.14 = (bf16[20,6,512]{2,1,0:T(8,128)(2,1)S(1)}, bf16[20,6,512]{2,1,0:T(8,128)(2,1)}, u32[]{:S(2)}) copy-start(bf16[20,6,512]{2,1,0:T(8,128)(2,1)} %copy-done.13) | copy-start | bytes 368644
  299.2 60.6 %collective-permute-start.25 = (f32[6,16,16]{1,0,2:T(8,128)}, f32[6,16,16]{1,0,2:T(8,128)}, u32[]{:S(2)}, u32[]{:S(2)}) collective-permute-start(f32[6,16,16]{1,0,2:T(8,128)} %slice.255), channel_id=1, source_target_pairs={{0,16},{16,32},{32,48},{48,64},{64,80},{80,96},{96,112},{112,128},... | collective-permute-start | bytes 18440 | tf_op jit(solution)/shard_map/ppermute | solution.py:18
  301.8 58.0 %collective-permute-start.26 = (f32[6,16,16]{1,0,2:T(8,128)}, f32[6,16,16]{1,0,2:T(8,128)}, u32[]{:S(2)}, u32[]{:S(2)}) collective-permute-start(f32[6,16,16]{1,0,2:T(8,128)} %slice.257), channel_id=1, source_target_pairs={{16,0},{32,16},{48,32},{64,48},{80,64},{96,80},{112,96},{128,112},... | collective-permute-start | bytes 18440 | tf_op jit(solution)/shard_map/ppermute | solution.py:21
  330.6 20.9 %copy-start = (bf16[20,28,512]{2,1,0:T(8,128)(2,1)S(1)}, bf16[20,28,512]{2,1,0:T(8,128)(2,1)}, u32[]{:S(2)}) copy-start(bf16[20,28,512]{2,1,0:T(8,128)(2,1)} %get-tuple-element.348) | copy-start | bytes 1720324
  331.3 35.1 %collective-permute-start.15 = (f32[6,16,16]{1,0,2:T(8,128)}, f32[6,16,16]{1,0,2:T(8,128)S(1)}, u32[]{:S(2)}, u32[]{:S(2)}) collective-permute-start(f32[6,16,16]{1,0,2:T(8,128)} %slice.233), channel_id=1, source_target_pairs={{0,16},{16,32},{32,48},{48,64},{64,80},{80,96},{96,112},{112,128},... | collective-permute-start | bytes 18440 | tf_op jit(solution)/shard_map/ppermute | solution.py:18
  334.0 32.5 %collective-permute-start.16 = (f32[6,16,16]{1,0,2:T(8,128)}, f32[6,16,16]{1,0,2:T(8,128)}, u32[]{:S(2)}, u32[]{:S(2)}) collective-permute-start(f32[6,16,16]{1,0,2:T(8,128)} %slice.235), channel_id=1, source_target_pairs={{16,0},{32,16},{48,32},{64,48},{80,64},{96,80},{112,96},{128,112},... | collective-permute-start | bytes 18440 | tf_op jit(solution)/shard_map/ppermute | solution.py:21
  359.0 7.4 %copy-start.24 = (f32[8,16,16]{1,0,2:T(8,128)S(1)}, f32[8,16,16]{1,0,2:T(8,128)}, u32[]{:S(2)}) copy-start(f32[8,16,16]{1,0,2:T(8,128)} %reshape.389) | copy-start | bytes 24580
  360.9 18.8 %collective-permute-start.27 = (f32[20,6,16]{1,0,2:T(8,128)S(1)}, f32[20,6,16]{1,0,2:T(8,128)S(1)}, u32[]{:S(2)}, u32[]{:S(2)}) collective-permute-start(f32[20,6,16]{1,0,2:T(8,128)S(1)} %get-tuple-element.322), channel_id=1, source_target_pairs={{0,1},{1,2},{2,3},{3,4},{4,5},{5,6},{6,7},{7,8},{8,9},{9,10},{10,1... | collective-permute-start | bytes 23048 | tf_op jit(solution)/shard_map/ppermute | solution.py:18
  362.8 16.8 %collective-permute-start.28 = (f32[20,6,16]{1,0,2:T(8,128)S(1)}, f32[20,6,16]{1,0,2:T(8,128)S(1)}, u32[]{:S(2)}, u32[]{:S(2)}) collective-permute-start(f32[20,6,16]{1,0,2:T(8,128)S(1)} %get-tuple-element.323), channel_id=1, source_target_pairs={{1,0},{2,1},{3,2},{4,3},{5,4},{6,5},{7,6},{8,7},{9,8},{10,9},{11,1... | collective-permute-start | bytes 23048 | tf_op jit(solution)/shard_map/ppermute | solution.py:21
  367.4 15.3 %collective-permute-start.17 = (f32[20,6,16]{1,0,2:T(8,128)S(1)}, f32[20,6,16]{1,0,2:T(8,128)S(1)}, u32[]{:S(2)}, u32[]{:S(2)}) collective-permute-start(f32[20,6,16]{1,0,2:T(8,128)S(1)} %get-tuple-element.326), channel_id=1, source_target_pairs={{0,1},{1,2},{2,3},{3,4},{4,5},{5,6},{6,7},{7,8},{8,9},{9,10},{10,1... | collective-permute-start | bytes 23048 | tf_op jit(solution)/shard_map/ppermute | solution.py:18
  369.4 13.3 %collective-permute-start.18 = (f32[20,6,16]{1,0,2:T(8,128)S(1)}, f32[20,6,16]{1,0,2:T(8,128)S(1)}, u32[]{:S(2)}, u32[]{:S(2)}) collective-permute-start(f32[20,6,16]{1,0,2:T(8,128)S(1)} %get-tuple-element.327), channel_id=1, source_target_pairs={{1,0},{2,1},{3,2},{4,3},{5,4},{6,5},{7,6},{8,7},{9,8},{10,9},{11,1... | collective-permute-start | bytes 23048 | tf_op jit(solution)/shard_map/ppermute | solution.py:21
  380.8 19.6 %collective-permute-start.29 = (f32[12,28,16]{1,0,2:T(8,128)S(1)}, f32[12,28,16]{1,0,2:T(8,128)S(1)}, u32[]{:S(2)}, u32[]{:S(2)}) collective-permute-start(f32[12,28,16]{1,0,2:T(8,128)S(1)} %pad_maximum_fusion.13), channel_id=1, source_target_pairs={{0,8},{8,0},{1,9},{9,1},{2,10},{10,2},{3,11},{11,3},{4,12},{12,4},... | collective-permute-start | bytes 64520 | tf_op jit(solution)/shard_map/ppermute | solution.py:41
  383.9 18.9 %collective-permute-start.19 = (f32[12,28,16]{1,0,2:T(8,128)S(1)}, f32[12,28,16]{1,0,2:T(8,128)S(1)}, u32[]{:S(2)}, u32[]{:S(2)}) collective-permute-start(f32[12,28,16]{1,0,2:T(8,128)S(1)} %pad_maximum_fusion.12), channel_id=1, source_target_pairs={{0,8},{8,0},{1,9},{9,1},{2,10},{10,2},{3,11},{11,3},{4,12},{12,4},... | collective-permute-start | bytes 64520 | tf_op jit(solution)/shard_map/ppermute | solution.py:41
  (20 other events, 31.5 us)
where the time goes:
time: 426 us; the launch traced here: 424 us
  starting transfers between devices  212 us (50%)
  waiting for transfers between devices  103 us (24%)
  local copies, waits for them, and re-layouts  58.7 us (14%)
  other arithmetic  27 us (6%)
  matrix products  20.7 us (5%)
    ppermute x12, starting transfers between devices, with_halo(): lax.ppermute(lax.slice_in_dim(block, 0, width, axis=dim), axis, backward)  141 us
    ppermute x6, waiting for transfers between devices, swapped(): return lax.ppermute(block, axis, route)  103 us
    ppermute x12, starting transfers between devices, with_halo(): lax.ppermute(lax.slice_in_dim(block, block.shape[dim] - width, None, axis...  42.8 us
    ppermute x6, starting transfers between devices, swapped(): return lax.ppermute(block, axis, route)  27.9 us
    unnamed x76, local copies, waits for them, and re-layouts  17.6 us
    select_n x6, local copies, waits for them, and re-layouts, splice(): return jnp.where(is_south, southern, padded)  14.7 us
    and x8, other arithmetic, neighbour_mask(): allowed & (jnp.logical_not(south_band)[None, None, :, None] | south_query...  9.31 us
  transfers between devices with their start and end apart: 30, of which 4 were waited for; matrix products, arithmetic and copies ran while one was open for 19% of the time, Pallas kernels for 0%

commit v1 on v0

v1 whole, which is shorter than its diff:
```python
import functools
import math

import jax
import jax.numpy as jnp
from jax import lax
from jax.experimental import pallas as pl
from jax.experimental.pallas import tpu as pltpu
from jax.sharding import PartitionSpec as P

HEAD_DIM = 32
RADIUS = 6
LANES = 128
GROUP = LANES // HEAD_DIM
EDGE = 8
MESH = pl.DeviceIdType.MESH
LOG2E = 1.4426950408889634
NEG = -1e30


def dot_nt(a, b):
    return lax.dot_general(a, b, (((1,), (1,)), ((), ())), preferred_element_type=jnp.float32)


def dot_nn(a, b):
    return lax.dot_general(a, b, (((1,), (0,)), ((), ())), preferred_element_type=jnp.float32)


def kernel(
    n_lat,
    n_lon,
    rows,
    cols,
    groups,
    q_ref,
    k_ref,
    v_ref,
    g_ref,
    reach_ref,
    dq_ref,
    dk_ref,
    dv_ref,
    field,
    stat,
    stat_own,
    bias,
    local_sem,
    lat_send,
    lat_recv,
    lon_send,
    lon_recv,
    stat_lat_send,
    stat_lat_recv,
    stat_lon_send,
    stat_lon_recv,
):
    lat, lon = lax.axis_index("lat"), lax.axis_index("lon")
    tall, wide = rows + 2 * RADIUS, cols + 2 * EDGE
    own, outer = rows * cols, tall * wide
    low = RADIUS + rows
    at_north = (n_lat - 1 - lat) // (n_lat - 1)
    at_south = lat // (n_lat - 1)
    up = (lat - 1 + at_north, (lon + at_north * (n_lon // 2)) % n_lon)
    down = (lat + 1 - at_south, (lon + at_south * (n_lon // 2)) % n_lon)
    up_slot, down_slot = 1 - at_north, at_south
    left = (lat, (lon + n_lon - 1) % n_lon)
    right = (lat, (lon + 1) % n_lon)

    sources = (k_ref, v_ref, q_ref, g_ref)

    def local_copy(g, a):
        return pltpu.make_async_copy(
            sources[a].at[:, :, pl.ds(g * LANES, LANES)],
            field.at[g, a, pl.ds(RADIUS, rows), pl.ds(EDGE, cols), :],
            local_sem.at[g, a],
        )

    for pair in range(2):
        for g in range(groups):
            for a in range(2):
                local_copy(g, 2 * pair + a).start()

    barrier = pltpu.get_barrier_semaphore()
    for device in (up, down, left, right):
        pl.semaphore_signal(barrier, inc=1, device_id=device, device_id_type=MESH)

    def lat_copy(pair, g, way):
        arrays = pl.ds(2 * pair, 2)
        slot = (up_slot, down_slot)[way]
        return pltpu.make_async_remote_copy(
            src_ref=field.at[g, arrays, pl.ds((RADIUS, rows)[way], RADIUS), pl.ds(EDGE, cols), :],
            dst_ref=field.at[g, arrays, pl.ds(slot * low, RADIUS), pl.ds(EDGE, cols), :],
            send_sem=lat_send.at[pair, g, way],
            recv_sem=lat_recv.at[pair, g, slot],
            device_id=(up, down)[way],
            device_id_type=MESH,
        )

    def lat_arrival(pair, g, slot):
        arrays = pl.ds(2 * pair, 2)
        there = field.at[g, arrays, pl.ds(slot * low, RADIUS), pl.ds(EDGE, cols), :]
        return pltpu.make_async_remote_copy(
            src_ref=there,
            dst_ref=there,
            send_sem=lat_send.at[pair, g, slot],
            recv_sem=lat_recv.at[pair, g, slot],
            device_id=up,
            device_id_type=MESH,
        )

    def lon_copy(pair, g, way):
        arrays = pl.ds(2 * pair, 2)
        return pltpu.make_async_remote_copy(
            src_ref=field.at[g, arrays, :, pl.ds((EDGE, cols)[way], EDGE), :],
            dst_ref=field.at[g, arrays, :, pl.ds((EDGE + cols, 0)[way], EDGE), :],
            send_sem=lon_send.at[pair, g, way],
            recv_sem=lon_recv.at[pair, g, way],
            device_id=(left, right)[way],
            device_id_type=MESH,
        )

    def stat_lat_copy(way):
        slot = (up_slot, down_slot)[way]
        return pltpu.make_async_remote_copy(
            src_ref=stat.at[pl.ds((RADIUS, rows)[way], RADIUS), pl.ds(EDGE, cols), :],
            dst_ref=stat.at[pl.ds(slot * low, RADIUS), pl.ds(EDGE, cols), :],
            send_sem=stat_lat_send.at[way],
            recv_sem=stat_lat_recv.at[slot],
            device_id=(up, down)[way],
            device_id_type=MESH,
        )

    def stat_lat_arrival(slot):
        there = stat.at[pl.ds(slot * low, RADIUS), pl.ds(EDGE, cols), :]
        return pltpu.make_async_remote_copy(
            src_ref=there,
            dst_ref=there,
            send_sem=stat_lat_send.at[slot],
            recv_sem=stat_lat_recv.at[slot],
            device_id=up,
            device_id_type=MESH,
        )

    def stat_lon_copy(way):
        return pltpu.make_async_remote_copy(
            src_ref=stat.at[:, pl.ds((EDGE, cols)[way], EDGE), :],
            dst_ref=stat.at[:, pl.ds((EDGE + cols, 0)[way], EDGE), :],
            send_sem=stat_lon_send.at[way],
            recv_sem=stat_lon_recv.at[way],
            device_id=(left, right)[way],
            device_id_type=MESH,
        )

    def send_lat(pair, g):
        for way in range(2):
            lat_copy(pair, g, way).start()

    pl.semaphore_wait(barrier, 4)
    for g in range(groups):
        for a in range(2):
            local_copy(g, a).wait()
        send_lat(0, g)
    for g in range(groups):
        for a in range(2, 4):
            local_copy(g, a).wait()
    send_lat(1, 0)

    total_cols = n_lon * cols
    reach = reach_ref[...].astype(jnp.float32)
    pick = lax.broadcasted_iota(jnp.int32, (16, total_cols), 0)
    table = jnp.where(
        pick == 0,
        jnp.broadcast_to(reach[0:1], (16, total_cols)),
        jnp.where(pick == 1, jnp.broadcast_to(reach[1:2], (16, total_cols)), 0.0),
    ).astype(jnp.bfloat16)
    outer_at = lax.broadcasted_iota(jnp.int32, (total_cols, outer), 1)
    outer_col = (lon * cols + outer_at % wide + (total_cols - EDGE + total_cols // 2)) % total_cols
    hit = lax.broadcasted_iota(jnp.int32, (total_cols, outer), 0) == outer_col
    key_reach = dot_nn(table, jnp.where(hit, 1.0, 0.0).astype(jnp.bfloat16))
    own_at = lax.broadcasted_iota(jnp.int32, (own, total_cols), 0)
    hit = lax.broadcasted_iota(jnp.int32, (own, total_cols), 1) == lon * cols + own_at % cols
    query_reach = dot_nt(jnp.where(hit, 1.0, 0.0).astype(jnp.bfloat16), table)
    k_at = lax.broadcasted_iota(jnp.int32, (1, outer), 1)
    k_row, k_col = k_at // wide, k_at % wide - EDGE
    k_north = (k_row < RADIUS) & (at_north == 1)
    k_south = (k_row >= low) & (at_south == 1)
    k_place = jnp.where(
        k_north, -1 - k_row, jnp.where(k_south, low + low - 1 - k_row, k_row - RADIUS)
    )
    k_depth = jnp.where(k_north, k_row, tall - 1 - k_row).astype(jnp.float32)
    k_polar = jnp.where(k_north, 1.0, jnp.where(k_south, 2.0, 0.0))
    k_ok = jnp.where(
        k_north,
        jnp.where(key_reach[0:1] > k_depth, 1.0, 0.0),
        jnp.where(k_south, jnp.where(key_reach[1:2] > k_depth, 1.0, 0.0), 1.0),
    )
    q_at = lax.broadcasted_iota(jnp.int32, (own, 1), 0)
    q_row, q_col = q_at // cols, q_at % cols
    q_north = jnp.where(query_reach[:, 0:1] > q_row.astype(jnp.float32), 1.0, 0.0)
    q_south = jnp.where(query_reach[:, 1:2] > (rows - 1 - q_row).astype(jnp.float32), 1.0, 0.0)
    near = (jnp.abs(k_place - q_row) <= RADIUS) & (jnp.abs(k_col - q_col) <= RADIUS)
    q_ok = jnp.where(k_polar == 1.0, q_north, jnp.where(k_polar == 2.0, q_south, 1.0))
    bias[...] = jnp.where(near & (q_ok * k_ok > 0.5), 0.0, NEG)

    lane = lax.broadcasted_iota(jnp.int32, (1, LANES), 1)
    in_head = [jnp.where(lane // HEAD_DIM == h, 1.0, 0.0) for h in range(GROUP)]
    in_head_half = [mask.astype(jnp.bfloat16) for mask in in_head]
    scale = 1.0 / math.sqrt(HEAD_DIM)
    to_log2 = scale * LOG2E

    def own_part(g, a):
        return field[g, a, pl.ds(RADIUS, rows), pl.ds(EDGE, cols), :].reshape(own, LANES)

    def outer_part(g, a):
        return field[g, a].reshape(outer, LANES)

    def features(g):
        return pl.ds(pl.multiple_of(g * LANES, LANES), LANES)

    stat_own[...] = jnp.zeros_like(stat_own)

    def query_step(g, carry):
        for slot in range(2):
            lat_arrival(0, g, slot).wait_recv()
        for way in range(2):
            lon_copy(0, g, way).start()
        query, grad = own_part(g, 2), own_part(g, 3)
        for way in range(2):
            lon_copy(0, g, way).wait_recv()
        key, value = outer_part(g, 0), outer_part(g, 1)
        query_grad = jnp.zeros((own, LANES), jnp.float32)
        stats = stat_own[...]
        for h in range(GROUP):
            grad_h = grad * in_head_half[h]
            logits = dot_nt(query * in_head_half[h], key) * to_log2 + bias[...]
            top = jnp.max(logits, axis=1, keepdims=True)
            weight = jnp.exp2(logits - top)
            total = jnp.sum(weight, axis=1, keepdims=True)
            probs = weight * (1.0 / total)
            attended = dot_nn(probs.astype(jnp.bfloat16), value)
            grad_dot = jnp.sum(grad_h.astype(jnp.float32) * attended, axis=1, keepdims=True)
            grad_probs = dot_nt(grad_h, value)
            grad_scores = (probs * (grad_probs - grad_dot)).astype(jnp.bfloat16)
            query_grad += dot_nn(grad_scores, key) * in_head[h]
            log_total = (top + jnp.log(total) * LOG2E) * (1.0 / to_log2)
            head = g * GROUP + h
            for part, stat_value in enumerate((log_total, grad_dot)):
                rest = -stat_value
                for piece in range(3):
                    kept = rest.astype(jnp.bfloat16).astype(jnp.float32)
                    rest = rest - kept
                    stats = jnp.where(lane == (3 * part + piece) * 16 + head, kept, stats)
        stat_own[...] = stats
        dq_ref[:, :, features(g)] = (
            (query_grad * scale).astype(jnp.bfloat16).reshape(rows, cols, LANES)
        )
        return carry

    lax.fori_loop(0, groups, query_step, 0)

    stat[pl.ds(RADIUS, rows), pl.ds(EDGE, cols), :] = (
        stat_own[...].astype(jnp.bfloat16).reshape(rows, cols, LANES)
    )
    for way in range(2):
        stat_lat_copy(way).start()
    for g in range(1, groups):
        send_lat(1, g)
    for slot in range(2):
        stat_lat_arrival(slot).wait_recv()
    for way in range(2):
        stat_lon_copy(way).start()

    def key_step(g, carry):
        for slot in range(2):
            lat_arrival(1, g, slot).wait_recv()
        for way in range(2):
            lon_copy(1, g, way).start()

        @pl.when(g == 0)
        def _():
            for way in range(2):
                stat_lon_copy(way).wait_recv()

        key, value = own_part(g, 0), own_part(g, 1)
        for way in range(2):
            lon_copy(1, g, way).wait_recv()
        query, grad = outer_part(g, 2), outer_part(g, 3)
        outer_stat = stat[...].reshape(outer, LANES)
        query_stat = jnp.concatenate([query, outer_stat], axis=1)
        grad_stat = jnp.concatenate([grad, outer_stat], axis=1)
        key_grad = jnp.zeros((own, LANES), jnp.float32)
        value_grad = jnp.zeros((own, LANES), jnp.float32)
        for h in range(GROUP):
            mine = lane % 16 == g * GROUP + h
            in_log = jnp.where(mine & (lane < 48), 1.0, 0.0).astype(jnp.bfloat16)
            in_dot = jnp.where(mine & (lane >= 48) & (lane < 96), 1.0, 0.0).astype(jnp.bfloat16)
            in_log = jnp.broadcast_to(in_log, (own, LANES))
            in_dot = jnp.broadcast_to(in_dot, (own, LANES))
            key_h = jnp.concatenate([key * in_head_half[h], in_log], axis=1)
            value_h = jnp.concatenate([value * in_head_half[h], in_dot], axis=1)
            probs = jnp.exp2(dot_nt(key_h, query_stat) * to_log2 + bias[...])
            value_grad += dot_nn(probs.astype(jnp.bfloat16), grad) * in_head[h]
            grad_scores = (probs * dot_nt(value_h, grad_stat)).astype(jnp.bfloat16)
            key_grad += dot_nn(grad_scores, query) * in_head[h]
        dk_ref[:, :, features(g)] = (
            (key_grad * scale).astype(jnp.bfloat16).reshape(rows, cols, LANES)
        )
        dv_ref[:, :, features(g)] = value_grad.astype(jnp.bfloat16).reshape(rows, cols, LANES)
        return carry

    lax.fori_loop(0, groups, key_step, 0)

    for way in range(2):
        for pair in range(2):
            for g in range(groups):
                lat_copy(pair, g, way).wait_send()
                lon_copy(pair, g, way).wait_send()
        stat_lat_copy(way).wait_send()
        stat_lon_copy(way).wait_send()


def shards(n_lat, n_lon, query_field, key_field, value_field, out_grad, pole_reach):
    rows, cols, width = query_field.shape
    groups = width // LANES
    tall, wide = rows + 2 * RADIUS, cols + 2 * EDGE
    shape = jax.ShapeDtypeStruct((rows, cols, width), jnp.bfloat16)
    dma = pltpu.SemaphoreType.DMA
    return pl.pallas_call(
        functools.partial(kernel, n_lat, n_lon, rows, cols, groups),
        out_shape=(shape, shape, shape),
        in_specs=[pl.BlockSpec(memory_space=pl.ANY)] * 4 + [pl.BlockSpec(memory_space=pltpu.VMEM)],
        out_specs=[pl.BlockSpec(memory_space=pltpu.VMEM)] * 3,
        scratch_shapes=[
            pltpu.VMEM((groups, 4, tall, wide, LANES), jnp.bfloat16),
            pltpu.VMEM((tall, wide, LANES), jnp.bfloat16),
            pltpu.VMEM((rows * cols, LANES), jnp.float32),
            pltpu.VMEM((rows * cols, tall * wide), jnp.float32),
            dma((groups, 4)),
            dma((2, groups, 2)),
            dma((2, groups, 2)),
            dma((2, groups, 2)),
            dma((2, groups, 2)),
            dma((2,)),
            dma((2,)),
            dma((2,)),
            dma((2,)),
        ],
        compiler_params=pltpu.CompilerParams(
            collective_id=0, has_side_effects=True, vmem_limit_bytes=40 << 20
        ),
    )(query_field, key_field, value_field, out_grad, pole_reach)


def solution(mesh):
    placed = P("lat", "lon", None)
    return jax.shard_map(
        functools.partial(shards, mesh.shape["lat"], mesh.shape["lon"]),
        mesh=mesh,
        in_specs=(placed, placed, placed, placed, P()),
        out_specs=(placed, placed, placed),
        check_vma=False,
    )
```

time: 426 us -> 174 us (0.41)
  the two profiles are of different devices: /device:TPU:1 before, /device:TPU:6 now
where the time goes in v1:
time: 174 us
  Pallas kernels  167 us (96%)
  local copies, waits for them, and re-layouts  6.26 us (4%)
    pallas_call x1, Pallas kernels, shards(): pl.pallas_call(functools.partial(kernel, n_lat, n_lon, rows, cols, groups...  167 us
    unnamed x13, local copies, waits for them, and re-layouts  6.26 us

profile of v1, /device:TPU:6, one launch (start us, length us, event | category | flops | bytes accessed | tf_op | source)
XLA Modules:
  0.0 173.6 jit_solution(3881254738585983192)
XLA Ops:
  0.6 0.0 copy-start
  0.6 0.9 copy-done
  1.5 0.0 copy-start.1
  1.5 0.9 copy-done.1
  2.4 0.0 copy-start.2
  2.4 0.9 copy-done.2
  3.3 0.0 copy-start.3
  3.3 0.9 copy-done.3
  4.3 0.0 copy-start.4
  4.3 0.7 copy-done.4
  4.9 166.7 %shard_map.76 = (bf16[8,16,512]{2,1,0:T(8,128)(2,1)S(1)}, bf16[8,16,512]{2,1,0:T(8,128)(2,1)S(1)}, bf16[8,16,512]{2,1,0:T(8,128)(2,1)S(1)}) custom-call(bf16[8,16,512]{2,1,0:T(8,128)(2,1)S(1)} %copy-done, bf16[8,16,512]{2,1,0:T(8,128)(2,1)S(1)} %copy-done.1, bf16[8,16,512]{2,1,0:T(8,128)(2,1)S(1)} %copy-done.2, bf16[8,16,512]{2,1,0:T(8,128)(2,1)S(1)} %copy-done.3, ...), custom_call_target="tpu_custom_call" | custom-call | tf_op jit(solution)/shard_map/pallas_call | solution.py:328
  171.6 0.7 copy.11
  172.3 0.7 copy.12
  173.0 0.7 copy.13
Async XLA Ops:
  0.6 0.9 copy-start
  1.5 0.9 copy-start.1
  2.4 0.9 copy-start.2
  3.3 0.9 copy-start.3
  4.3 0.7 copy-start.4

commit v2 on v1

--- a/solution.py
+++ b/solution.py
@@ -36,7 +36,7 @@
     k_ref,
     v_ref,
     g_ref,
-    reach_ref,
+    reach_hbm,
     dq_ref,
     dk_ref,
     dv_ref,
@@ -44,11 +44,19 @@
     stat,
     stat_own,
     bias,
+    reach_ref,
+    reach_sem,
     local_sem,
     lat_send,
     lat_recv,
     lon_send,
     lon_recv,
+    lon_own_send,
+    lon_own_recv,
+    relayed,
+    relay_send,
+    relay_recv,
+    relay_on_send,
     stat_lat_send,
     stat_lat_recv,
     stat_lon_send,
@@ -57,7 +65,7 @@
     lat, lon = lax.axis_index("lat"), lax.axis_index("lon")
     tall, wide = rows + 2 * RADIUS, cols + 2 * EDGE
     own, outer = rows * cols, tall * wide
-    low = RADIUS + rows
+    own_rows, halo_rows = pl.ds(0, rows), pl.ds(rows, 2 * RADIUS)
     at_north = (n_lat - 1 - lat) // (n_lat - 1)
     at_south = lat // (n_lat - 1)
     up = (lat - 1 + at_north, (lon + at_north * (n_lon // 2)) % n_lon)
@@ -71,7 +79,7 @@
     def local_copy(g, a):
         return pltpu.make_async_copy(
             sources[a].at[:, :, pl.ds(g * LANES, LANES)],
-            field.at[g, a, pl.ds(RADIUS, rows), pl.ds(EDGE, cols), :],
+            field.at[g, a, own_rows, pl.ds(EDGE, cols), :],
             local_sem.at[g, a],
         )
 
@@ -80,16 +88,71 @@
             for a in range(2):
                 local_copy(g, 2 * pair + a).start()
 
+    reach_copy = pltpu.make_async_copy(reach_hbm, reach_ref, reach_sem)
+    reach_copy.start()
+
+    half_lon = n_lon // 2
+    half = lon // half_lon
+    north_relay, south_relay = n_lat - 4, 3
+    north_source, south_source = at_north * (1 - half), at_south * half
+    in_north_relay = (lat == north_relay) & (half == 0)
+    in_south_relay = (lat == south_relay) & (half == 1)
+    relay = (
+        at_north * north_relay + at_south * south_relay,
+        lon % half_lon + at_south * half_lon,
+    )
+    relay_ends = (
+        ((0, lon), (0, (lon + half_lon) % n_lon)),
+        ((n_lat - 1, lon), (n_lat - 1, (lon + half_lon) % n_lon)),
+    )
+
     barrier = pltpu.get_barrier_semaphore()
+
+    def greet(device):
+        pl.semaphore_signal(barrier, inc=1, device_id=device, device_id_type=MESH)
+
     for device in (up, down, left, right):
-        pl.semaphore_signal(barrier, inc=1, device_id=device, device_id_type=MESH)
+        greet(device)
+
+    @pl.when(at_north + at_south == 1)
+    def _():
+        greet(relay)
+
+    for inside, ends in zip((in_north_relay, in_south_relay), relay_ends):
+
+        @pl.when(inside)
+        def _(ends=ends):
+            for device in ends:
+                greet(device)
+
+    def relay_copy(pair, way):
+        arrays = pl.ds(2 * pair, 2)
+        return pltpu.make_async_remote_copy(
+            src_ref=field.at[:, arrays, pl.ds((0, rows - RADIUS)[way], RADIUS), pl.ds(EDGE, cols), :],
+            dst_ref=relayed.at[:, arrays],
+            send_sem=relay_send.at[pair],
+            recv_sem=relay_recv.at[pair],
+            device_id=relay,
+            device_id_type=MESH,
+        )
+
+    def relay_on(pair, g, slot):
+        arrays = pl.ds(2 * pair, 2)
+        return pltpu.make_async_remote_copy(
+            src_ref=relayed.at[g, arrays],
+            dst_ref=field.at[g, arrays, pl.ds(rows + slot * RADIUS, RADIUS), pl.ds(EDGE, cols), :],
+            send_sem=relay_on_send.at[pair, g],
+            recv_sem=lat_recv.at[pair, g, slot],
+            device_id=relay_ends[slot][1],
+            device_id_type=MESH,
+        )
 
     def lat_copy(pair, g, way):
         arrays = pl.ds(2 * pair, 2)
         slot = (up_slot, down_slot)[way]
         return pltpu.make_async_remote_copy(
-            src_ref=field.at[g, arrays, pl.ds((RADIUS, rows)[way], RADIUS), pl.ds(EDGE, cols), :],
-            dst_ref=field.at[g, arrays, pl.ds(slot * low, RADIUS), pl.ds(EDGE, cols), :],
+            src_ref=field.at[g, arrays, pl.ds((0, rows - RADIUS)[way], RADIUS), pl.ds(EDGE, cols), :],
+            dst_ref=field.at[g, arrays, pl.ds(rows + slot * RADIUS, RADIUS), pl.ds(EDGE, cols), :],
             send_sem=lat_send.at[pair, g, way],
             recv_sem=lat_recv.at[pair, g, slot],
             device_id=(up, down)[way],
@@ -98,7 +161,7 @@
 
     def lat_arrival(pair, g, slot):
         arrays = pl.ds(2 * pair, 2)
-        there = field.at[g, arrays, pl.ds(slot * low, RADIUS), pl.ds(EDGE, cols), :]
+        there = field.at[g, arrays, pl.ds(rows + slot * RADIUS, RADIUS), pl.ds(EDGE, cols), :]
         return pltpu.make_async_remote_copy(
             src_ref=there,
             dst_ref=there,
@@ -111,19 +174,30 @@
     def lon_copy(pair, g, way):
         arrays = pl.ds(2 * pair, 2)
         return pltpu.make_async_remote_copy(
-            src_ref=field.at[g, arrays, :, pl.ds((EDGE, cols)[way], EDGE), :],
-            dst_ref=field.at[g, arrays, :, pl.ds((EDGE + cols, 0)[way], EDGE), :],
+            src_ref=field.at[g, arrays, halo_rows, pl.ds((EDGE, cols)[way], EDGE), :],
+            dst_ref=field.at[g, arrays, halo_rows, pl.ds((EDGE + cols, 0)[way], EDGE), :],
             send_sem=lon_send.at[pair, g, way],
             recv_sem=lon_recv.at[pair, g, way],
             device_id=(left, right)[way],
             device_id_type=MESH,
         )
 
+    def lon_own_copy(pair, way):
+        arrays = pl.ds(2 * pair, 2)
+        return pltpu.make_async_remote_copy(
+            src_ref=field.at[:, arrays, own_rows, pl.ds((EDGE, cols)[way], EDGE), :],
+            dst_ref=field.at[:, arrays, own_rows, pl.ds((EDGE + cols, 0)[way], EDGE), :],
+            send_sem=lon_own_send.at[pair, way],
+            recv_sem=lon_own_recv.at[pair, way],
+            device_id=(left, right)[way],
+            device_id_type=MESH,
+        )
+
     def stat_lat_copy(way):
         slot = (up_slot, down_slot)[way]
         return pltpu.make_async_remote_copy(
-            src_ref=stat.at[pl.ds((RADIUS, rows)[way], RADIUS), pl.ds(EDGE, cols), :],
-            dst_ref=stat.at[pl.ds(slot * low, RADIUS), pl.ds(EDGE, cols), :],
+            src_ref=stat.at[pl.ds((0, rows - RADIUS)[way], RADIUS), pl.ds(EDGE, cols), :],
+            dst_ref=stat.at[pl.ds(rows + slot * RADIUS, RADIUS), pl.ds(EDGE, cols), :],
             send_sem=stat_lat_send.at[way],
             recv_sem=stat_lat_recv.at[slot],
             device_id=(up, down)[way],
@@ -131,7 +205,7 @@
         )
 
     def stat_lat_arrival(slot):
-        there = stat.at[pl.ds(slot * low, RADIUS), pl.ds(EDGE, cols), :]
+        there = stat.at[pl.ds(rows + slot * RADIUS, RADIUS), pl.ds(EDGE, cols), :]
         return pltpu.make_async_remote_copy(
             src_ref=there,
             dst_ref=there,
@@ -141,29 +215,61 @@
             device_id_type=MESH,
         )
 
-    def stat_lon_copy(way):
-        return pltpu.make_async_remote_copy(
-            src_ref=stat.at[:, pl.ds((EDGE, cols)[way], EDGE), :],
-            dst_ref=stat.at[:, pl.ds((EDGE + cols, 0)[way], EDGE), :],
-            send_sem=stat_lon_send.at[way],
-            recv_sem=stat_lon_recv.at[way],
+    def stat_lon_copy(part, way):
+        span = (own_rows, halo_rows)[part]
+        return pltpu.make_async_remote_copy(
+            src_ref=stat.at[span, pl.ds((EDGE, cols)[way], EDGE), :],
+            dst_ref=stat.at[span, pl.ds((EDGE + cols, 0)[way], EDGE), :],
+            send_sem=stat_lon_send.at[part, way],
+            recv_sem=stat_lon_recv.at[part, way],
             device_id=(left, right)[way],
             device_id_type=MESH,
         )
 
-    def send_lat(pair, g):
-        for way in range(2):
-            lat_copy(pair, g, way).start()
-
-    pl.semaphore_wait(barrier, 4)
+    def each_lat(chunks, act):
+        for skipped, ways in ((north_source, (1,)), (south_source, (0,)), (None, (0, 1))):
+            here = north_source + south_source == 0 if skipped is None else skipped == 1
+
+            @pl.when(here)
+            def _(ways=ways):
+                for pair, g in chunks:
+                    for way in ways:
+                        act(lat_copy(pair, g, way))
+
+    def start(copy):
+        copy.start()
+
+    def wait_send(copy):
+        copy.wait_send()
+
     for g in range(groups):
-        for a in range(2):
+        for a in range(4):
             local_copy(g, a).wait()
-        send_lat(0, g)
-    for g in range(groups):
-        for a in range(2, 4):
-            local_copy(g, a).wait()
-    send_lat(1, 0)
+    polar, relaying = at_north + at_south == 1, in_north_relay | in_south_relay
+    for here, peers in (
+        (polar, 5),
+        (relaying, 6),
+        (jnp.logical_not(polar | relaying), 4),
+    ):
+
+        @pl.when(here)
+        def _(peers=peers):
+            pl.semaphore_wait(barrier, peers)
+
+    for way, source in enumerate((north_source, south_source)):
+
+        @pl.when(source == 1)
+        def _(way=way):
+            for pair in range(2):
+                relay_copy(pair, way).start()
+
+    for way in range(2):
+        lon_own_copy(0, way).start()
+    ahead = groups // 2
+    each_lat([(0, g) for g in range(groups)] + [(1, g) for g in range(ahead)], start)
+    for way in range(2):
+        lon_own_copy(1, way).start()
+    reach_copy.wait()
 
     total_cols = n_lon * cols
     reach = reach_ref[...].astype(jnp.float32)
@@ -182,12 +288,15 @@
     query_reach = dot_nt(jnp.where(hit, 1.0, 0.0).astype(jnp.bfloat16), table)
     k_at = lax.broadcasted_iota(jnp.int32, (1, outer), 1)
     k_row, k_col = k_at // wide, k_at % wide - EDGE
-    k_north = (k_row < RADIUS) & (at_north == 1)
-    k_south = (k_row >= low) & (at_south == 1)
+    k_above, k_below = k_row - rows, k_row - rows - RADIUS
+    k_north = (k_above >= 0) & (k_below < 0) & (at_north == 1)
+    k_south = (k_below >= 0) & (at_south == 1)
     k_place = jnp.where(
-        k_north, -1 - k_row, jnp.where(k_south, low + low - 1 - k_row, k_row - RADIUS)
+        k_below >= 0,
+        jnp.where(k_south, rows + RADIUS - 1 - k_below, rows + k_below),
+        jnp.where(k_above >= 0, jnp.where(k_north, -1 - k_above, k_above - RADIUS), k_row),
     )
-    k_depth = jnp.where(k_north, k_row, tall - 1 - k_row).astype(jnp.float32)
+    k_depth = jnp.where(k_north, k_above, RADIUS - 1 - k_below).astype(jnp.float32)
     k_polar = jnp.where(k_north, 1.0, jnp.where(k_south, 2.0, 0.0))
     k_ok = jnp.where(
         k_north,
@@ -209,7 +318,7 @@
     to_log2 = scale * LOG2E
 
     def own_part(g, a):
-        return field[g, a, pl.ds(RADIUS, rows), pl.ds(EDGE, cols), :].reshape(own, LANES)
+        return field[g, a, own_rows, pl.ds(EDGE, cols), :].reshape(own, LANES)
 
     def outer_part(g, a):
         return field[g, a].reshape(outer, LANES)
@@ -219,11 +328,31 @@
 
     stat_own[...] = jnp.zeros_like(stat_own)
 
+    for slot, inside in enumerate((in_north_relay, in_south_relay)):
+
+        @pl.when(inside)
+        def _(slot=slot):
+            for pair in range(2):
+                relay_copy(pair, slot).wait_recv()
+                for g in range(groups):
+                    relay_on(pair, g, slot).start()
+
+
+    def pass_on(pair, g):
+        for slot in range(2):
+            lat_arrival(pair, g, slot).wait_recv()
+        for way in range(2):
+            lon_copy(pair, g, way).start()
+
+    pass_on(0, 0)
+    for way in range(2):
+        lon_own_copy(0, way).wait_recv()
+
     def query_step(g, carry):
-        for slot in range(2):
-            lat_arrival(0, g, slot).wait_recv()
-        for way in range(2):
-            lon_copy(0, g, way).start()
+        @pl.when(g + 1 < groups)
+        def _():
+            pass_on(0, g + 1)
+
         query, grad = own_part(g, 2), own_part(g, 3)
         for way in range(2):
             lon_copy(0, g, way).wait_recv()
@@ -258,28 +387,32 @@
 
     lax.fori_loop(0, groups, query_step, 0)
 
-    stat[pl.ds(RADIUS, rows), pl.ds(EDGE, cols), :] = (
+    stat[own_rows, pl.ds(EDGE, cols), :] = (
         stat_own[...].astype(jnp.bfloat16).reshape(rows, cols, LANES)
     )
     for way in range(2):
         stat_lat_copy(way).start()
-    for g in range(1, groups):
-        send_lat(1, g)
+        stat_lon_copy(0, way).start()
+    each_lat([(1, g) for g in range(ahead, groups)], start)
+    for g in range(ahead):
+        pass_on(1, g)
     for slot in range(2):
         stat_lat_arrival(slot).wait_recv()
     for way in range(2):
-        stat_lon_copy(way).start()
+        stat_lon_copy(1, way).start()
+    for way in range(2):
+        lon_own_copy(1, way).wait_recv()
 
     def key_step(g, carry):
-        for slot in range(2):
-            lat_arrival(1, g, slot).wait_recv()
-        for way in range(2):
-            lon_copy(1, g, way).start()
+        @pl.when(g + ahead < groups)
+        def _():
+            pass_on(1, g + ahead)
 
         @pl.when(g == 0)
         def _():
-            for way in range(2):
-                stat_lon_copy(way).wait_recv()
+            for part in range(2):
+                for way in range(2):
+                    stat_lon_copy(part, way).wait_recv()
 
         key, value = own_part(g, 0), own_part(g, 1)
         for way in range(2):
@@ -310,13 +443,30 @@
 
     lax.fori_loop(0, groups, key_step, 0)
 
+    each_lat([(pair, g) for pair in range(2) for g in range(groups)], wait_send)
+    for way, source in enumerate((north_source, south_source)):
+
+        @pl.when(source == 1)
+        def _(way=way):
+            for pair in range(2):
+                relay_copy(pair, way).wait_send()
+
+    for slot, inside in enumerate((in_north_relay, in_south_relay)):
+
+        @pl.when(inside)
+        def _(slot=slot):
+            for pair in range(2):
+                for g in range(groups):
+                    relay_on(pair, g, slot).wait_send()
+
     for way in range(2):
         for pair in range(2):
             for g in range(groups):
-                lat_copy(pair, g, way).wait_send()
                 lon_copy(pair, g, way).wait_send()
+            lon_own_copy(pair, way).wait_send()
         stat_lat_copy(way).wait_send()
-        stat_lon_copy(way).wait_send()
+        for part in range(2):
+            stat_lon_copy(part, way).wait_send()
 
 
 def shards(n_lat, n_lon, query_field, key_field, value_field, out_grad, pole_reach):
@@ -328,25 +478,33 @@
     return pl.pallas_call(
         functools.partial(kernel, n_lat, n_lon, rows, cols, groups),
         out_shape=(shape, shape, shape),
-        in_specs=[pl.BlockSpec(memory_space=pl.ANY)] * 4 + [pl.BlockSpec(memory_space=pltpu.VMEM)],
+        in_specs=[pl.BlockSpec(memory_space=pltpu.HBM)] * 5,
         out_specs=[pl.BlockSpec(memory_space=pltpu.VMEM)] * 3,
         scratch_shapes=[
             pltpu.VMEM((groups, 4, tall, wide, LANES), jnp.bfloat16),
             pltpu.VMEM((tall, wide, LANES), jnp.bfloat16),
             pltpu.VMEM((rows * cols, LANES), jnp.float32),
             pltpu.VMEM((rows * cols, tall * wide), jnp.float32),
+            pltpu.VMEM(pole_reach.shape, jnp.int32),
+            dma,
             dma((groups, 4)),
             dma((2, groups, 2)),
             dma((2, groups, 2)),
             dma((2, groups, 2)),
             dma((2, groups, 2)),
+            dma((2, 2)),
+            dma((2, 2)),
+            pltpu.VMEM((groups, 4, RADIUS, cols, LANES), jnp.bfloat16),
             dma((2,)),
             dma((2,)),
+            dma((2, groups)),
             dma((2,)),
             dma((2,)),
+            dma((2, 2)),
+            dma((2, 2)),
         ],
         compiler_params=pltpu.CompilerParams(
-            collective_id=0, has_side_effects=True, vmem_limit_bytes=40 << 20
+            collective_id=0, has_side_effects=True, vmem_limit_bytes=60 << 20
         ),
     )(query_field, key_field, value_field, out_grad, pole_reach)
 

time: 174 us -> 143 us (0.82)
  the two profiles are of different devices: /device:TPU:6 before, /device:TPU:256 now
where the time goes in v2:
time: 143 us
  Pallas kernels  139 us (97%)
  local copies, waits for them, and re-layouts  3.21 us (2%)
    pallas_call x1, Pallas kernels, shards(): pl.pallas_call(functools.partial(kernel, n_lat, n_lon, rows, cols, groups...  139 us
    unnamed x7, local copies, waits for them, and re-layouts  3.21 us

profile of v2, /device:TPU:256, one launch (start us, length us, event | category | flops | bytes accessed | tf_op | source)
XLA Modules:
  0.0 142.6 jit_solution(16199411599444479925)
XLA Ops:
  0.6 138.8 %shard_map.76 = (bf16[8,16,512]{2,1,0:T(8,128)(2,1)}, bf16[8,16,512]{2,1,0:T(8,128)(2,1)}, bf16[8,16,512]{2,1,0:T(8,128)(2,1)}) custom-call(bf16[8,16,512]{2,1,0:T(8,128)(2,1)} %q_ref.1, bf16[8,16,512]{2,1,0:T(8,128)(2,1)} %k_ref.1, bf16[8,16,512]{2,1,0:T(8,128)(2,1)} %v_ref.1, bf16[8,16,512]{2,1,0:T(8,128)(2,1)} %g_ref.1, s32[2,256]{1,0:T(2,128)} %reach_hbm.1), custom_call_target="tpu_custom_call" | custom-call | tf_op jit(solution)/shard_map/pallas_call | solution.py:478
  139.4 0.0 copy-start.1
  139.4 1.6 %copy.11 = bf16[8,16,512]{2,1,0:T(8,128)(2,1)} copy(bf16[8,16,512]{2,1,0:T(8,128)(2,1)} %get-tuple-element.6) | data formatting | bytes 262144
  141.0 0.0 copy-done.1
  141.0 0.0 copy-start
  141.0 0.7 copy.12
  141.7 0.3 copy-done
  142.0 0.7 copy.13
Async XLA Ops:
  139.4 1.6 %copy-start.1 = (bf16[8,16,512]{2,1,0:T(8,128)(2,1)S(1)}, bf16[8,16,512]{2,1,0:T(8,128)(2,1)}, u32[]{:S(2)}) copy-start(bf16[8,16,512]{2,1,0:T(8,128)(2,1)} %get-tuple-element.7) | copy-start | bytes 393220
  141.0 1.0 copy-start

commit v3 on v2

--- a/solution.py
+++ b/solution.py
@@ -37,10 +37,14 @@
     v_ref,
     g_ref,
     reach_hbm,
+    dq_hbm,
+    dk_hbm,
+    dv_hbm,
+    field,
     dq_ref,
     dk_ref,
     dv_ref,
-    field,
+    out_sem,
     stat,
     stat_own,
     bias,
@@ -265,8 +269,7 @@
 
     for way in range(2):
         lon_own_copy(0, way).start()
-    ahead = groups // 2
-    each_lat([(0, g) for g in range(groups)] + [(1, g) for g in range(ahead)], start)
+    each_lat([(0, g) for g in range(groups)], start)
     for way in range(2):
         lon_own_copy(1, way).start()
     reach_copy.wait()
@@ -326,6 +329,14 @@
     def features(g):
         return pl.ds(pl.multiple_of(g * LANES, LANES), LANES)
 
+    results = ((dq_ref, dq_hbm), (dk_ref, dk_hbm), (dv_ref, dv_hbm))
+
+    def out_copy(g, which):
+        held, result = results[which]
+        return pltpu.make_async_copy(
+            held.at[g], result.at[:, :, features(g)], out_sem.at[which, g]
+        )
+
     stat_own[...] = jnp.zeros_like(stat_own)
 
     for slot, inside in enumerate((in_north_relay, in_south_relay)):
@@ -352,6 +363,12 @@
         @pl.when(g + 1 < groups)
         def _():
             pass_on(0, g + 1)
+
+        for c in range(groups - 1):
+
+            @pl.when(g == c)
+            def _(c=c):
+                each_lat([(1, c)], start)
 
         query, grad = own_part(g, 2), own_part(g, 3)
         for way in range(2):
@@ -380,9 +397,8 @@
                     rest = rest - kept
                     stats = jnp.where(lane == (3 * part + piece) * 16 + head, kept, stats)
         stat_own[...] = stats
-        dq_ref[:, :, features(g)] = (
-            (query_grad * scale).astype(jnp.bfloat16).reshape(rows, cols, LANES)
-        )
+        dq_ref[g] = (query_grad * scale).astype(jnp.bfloat16).reshape(rows, cols, LANES)
+        out_copy(g, 0).start()
         return carry
 
     lax.fori_loop(0, groups, query_step, 0)
@@ -393,7 +409,8 @@
     for way in range(2):
         stat_lat_copy(way).start()
         stat_lon_copy(0, way).start()
-    each_lat([(1, g) for g in range(ahead, groups)], start)
+    each_lat([(1, groups - 1)], start)
+    ahead = groups // 2
     for g in range(ahead):
         pass_on(1, g)
     for slot in range(2):
@@ -435,15 +452,18 @@
             value_grad += dot_nn(probs.astype(jnp.bfloat16), grad) * in_head[h]
             grad_scores = (probs * dot_nt(value_h, grad_stat)).astype(jnp.bfloat16)
             key_grad += dot_nn(grad_scores, query) * in_head[h]
-        dk_ref[:, :, features(g)] = (
-            (key_grad * scale).astype(jnp.bfloat16).reshape(rows, cols, LANES)
-        )
-        dv_ref[:, :, features(g)] = value_grad.astype(jnp.bfloat16).reshape(rows, cols, LANES)
+        dk_ref[g] = (key_grad * scale).astype(jnp.bfloat16).reshape(rows, cols, LANES)
+        out_copy(g, 1).start()
+        dv_ref[g] = value_grad.astype(jnp.bfloat16).reshape(rows, cols, LANES)
+        out_copy(g, 2).start()
         return carry
 
     lax.fori_loop(0, groups, key_step, 0)
 
     each_lat([(pair, g) for pair in range(2) for g in range(groups)], wait_send)
+    for g in range(groups):
+        for which in range(3):
+            out_copy(g, which).wait()
     for way, source in enumerate((north_source, south_source)):
 
         @pl.when(source == 1)
@@ -469,19 +489,32 @@
             stat_lon_copy(part, way).wait_send()
 
 
+def copy_kernel(a, b, c, a_out, b_out, c_out, sem):
+    pairs = ((a, a_out), (b, b_out), (c, c_out))
+    copies = [pltpu.make_async_copy(x, y, sem.at[i]) for i, (x, y) in enumerate(pairs)]
+    for copy in copies:
+        copy.start()
+    for copy in copies:
+        copy.wait()
+
+
 def shards(n_lat, n_lon, query_field, key_field, value_field, out_grad, pole_reach):
     rows, cols, width = query_field.shape
     groups = width // LANES
     tall, wide = rows + 2 * RADIUS, cols + 2 * EDGE
     shape = jax.ShapeDtypeStruct((rows, cols, width), jnp.bfloat16)
     dma = pltpu.SemaphoreType.DMA
-    return pl.pallas_call(
+    results = pl.pallas_call(
         functools.partial(kernel, n_lat, n_lon, rows, cols, groups),
         out_shape=(shape, shape, shape),
         in_specs=[pl.BlockSpec(memory_space=pltpu.HBM)] * 5,
-        out_specs=[pl.BlockSpec(memory_space=pltpu.VMEM)] * 3,
+        out_specs=[pl.BlockSpec(memory_space=pltpu.HBM)] * 3,
         scratch_shapes=[
             pltpu.VMEM((groups, 4, tall, wide, LANES), jnp.bfloat16),
+            pltpu.VMEM((groups, rows, cols, LANES), jnp.bfloat16),
+            pltpu.VMEM((groups, rows, cols, LANES), jnp.bfloat16),
+            pltpu.VMEM((groups, rows, cols, LANES), jnp.bfloat16),
+            dma((3, groups)),
             pltpu.VMEM((tall, wide, LANES), jnp.bfloat16),
             pltpu.VMEM((rows * cols, LANES), jnp.float32),
             pltpu.VMEM((rows * cols, tall * wide), jnp.float32),
@@ -507,6 +540,14 @@
             collective_id=0, has_side_effects=True, vmem_limit_bytes=60 << 20
         ),
     )(query_field, key_field, value_field, out_grad, pole_reach)
+    return pl.pallas_call(
+        copy_kernel,
+        out_shape=(shape, shape, shape),
+        in_specs=[pl.BlockSpec(memory_space=pltpu.HBM)] * 3,
+        out_specs=[pl.BlockSpec(memory_space=pltpu.HBM)] * 3,
+        scratch_shapes=[dma((3,))],
+        compiler_params=pltpu.CompilerParams(vmem_limit_bytes=60 << 20),
+    )(*results)
 
 
 def solution(mesh):

time: 143 us -> 150 us (1.049)
  Pallas kernels: 139 us -> 149 us
  local copies, waits for them, and re-layouts: 3.21 us -> 0 us
    pallas_call x0 -> x1, Pallas kernels: none -> 13 us  [shards(): pl.pallas_call(copy_kernel, out_shape=(shape, shape, shape), in_specs=[pl...]
    unnamed x7 -> x0, local copies, waits for them, and re-layouts: 3.21 us -> none
    pallas_call x1, Pallas kernels: 139 us -> 136 us  [shards(): pl.pallas_call(functools.partial(kernel, n_lat, n_lon, rows, cols, groups...]
where the time goes in v3:
time: 150 us
  Pallas kernels  149 us (99%)
    pallas_call x1, Pallas kernels, shards(): pl.pallas_call(functools.partial(kernel, n_lat, n_lon, rows, cols, groups...  136 us
    pallas_call x1, Pallas kernels, shards(): pl.pallas_call(copy_kernel, out_shape=(shape, shape, shape), in_specs=[pl...  13 us

profile of v3, /device:TPU:256, one launch (start us, length us, event | category | flops | bytes accessed | tf_op | source)
XLA Modules:
  0.0 149.6 jit_solution(3566489456340677405)
XLA Ops:
  0.6 135.9 %shard_map.76 = (bf16[8,16,512]{2,1,0:T(8,128)(2,1)}, bf16[8,16,512]{2,1,0:T(8,128)(2,1)}, bf16[8,16,512]{2,1,0:T(8,128)(2,1)}) custom-call(bf16[8,16,512]{2,1,0:T(8,128)(2,1)} %q_ref.1, bf16[8,16,512]{2,1,0:T(8,128)(2,1)} %k_ref.1, bf16[8,16,512]{2,1,0:T(8,128)(2,1)} %v_ref.1, bf16[8,16,512]{2,1,0:T(8,128)(2,1)} %g_ref.1, s32[2,256]{1,0:T(2,128)} %reach_hbm.1), custom_call_target="tpu_custom_call" | custom-call | tf_op jit(solution)/shard_map/pallas_call | solution.py:507
  136.5 13.0 %shard_map.77 = (bf16[8,16,512]{2,1,0:T(8,128)(2,1)}, bf16[8,16,512]{2,1,0:T(8,128)(2,1)}, bf16[8,16,512]{2,1,0:T(8,128)(2,1)}) custom-call(bf16[8,16,512]{2,1,0:T(8,128)(2,1)} %get-tuple-element.6.a, bf16[8,16,512]{2,1,0:T(8,128)(2,1)} %get-tuple-element.7.b, bf16[8,16,512]{2,1,0:T(8,128)(2,1)} %get-tuple-element.8.c), custom_call_target="tpu_custom_call" | custom-call | tf_op jit(solution)/shard_map/pallas_call | solution.py:543

commit v4 on v3

--- a/solution.py
+++ b/solution.py
@@ -110,6 +110,10 @@
         ((n_lat - 1, lon), (n_lat - 1, (lon + half_lon) % n_lon)),
     )
 
+    for edge in (pl.ds(0, EDGE), pl.ds(EDGE + cols, EDGE)):
+        field[:, :, :, edge, :] = jnp.zeros((groups, 4, tall, EDGE, LANES), jnp.bfloat16)
+        stat[:, edge, :] = jnp.zeros((tall, EDGE, LANES), jnp.bfloat16)
+
     barrier = pltpu.get_barrier_semaphore()
 
     def greet(device):
@@ -178,8 +182,8 @@
     def lon_copy(pair, g, way):
         arrays = pl.ds(2 * pair, 2)
         return pltpu.make_async_remote_copy(
-            src_ref=field.at[g, arrays, halo_rows, pl.ds((EDGE, cols)[way], EDGE), :],
-            dst_ref=field.at[g, arrays, halo_rows, pl.ds((EDGE + cols, 0)[way], EDGE), :],
+            src_ref=field.at[g, arrays, halo_rows, pl.ds((EDGE, EDGE + cols - RADIUS)[way], RADIUS), :],
+            dst_ref=field.at[g, arrays, halo_rows, pl.ds((EDGE + cols, EDGE - RADIUS)[way], RADIUS), :],
             send_sem=lon_send.at[pair, g, way],
             recv_sem=lon_recv.at[pair, g, way],
             device_id=(left, right)[way],
@@ -189,8 +193,8 @@
     def lon_own_copy(pair, way):
         arrays = pl.ds(2 * pair, 2)
         return pltpu.make_async_remote_copy(
-            src_ref=field.at[:, arrays, own_rows, pl.ds((EDGE, cols)[way], EDGE), :],
-            dst_ref=field.at[:, arrays, own_rows, pl.ds((EDGE + cols, 0)[way], EDGE), :],
+            src_ref=field.at[:, arrays, own_rows, pl.ds((EDGE, EDGE + cols - RADIUS)[way], RADIUS), :],
+            dst_ref=field.at[:, arrays, own_rows, pl.ds((EDGE + cols, EDGE - RADIUS)[way], RADIUS), :],
             send_sem=lon_own_send.at[pair, way],
             recv_sem=lon_own_recv.at[pair, way],
             device_id=(left, right)[way],
@@ -222,8 +226,8 @@
     def stat_lon_copy(part, way):
         span = (own_rows, halo_rows)[part]
         return pltpu.make_async_remote_copy(
-            src_ref=stat.at[span, pl.ds((EDGE, cols)[way], EDGE), :],
-            dst_ref=stat.at[span, pl.ds((EDGE + cols, 0)[way], EDGE), :],
+            src_ref=stat.at[span, pl.ds((EDGE, EDGE + cols - RADIUS)[way], RADIUS), :],
+            dst_ref=stat.at[span, pl.ds((EDGE + cols, EDGE - RADIUS)[way], RADIUS), :],
             send_sem=stat_lon_send.at[part, way],
             recv_sem=stat_lon_recv.at[part, way],
             device_id=(left, right)[way],
@@ -489,12 +493,16 @@
             stat_lon_copy(part, way).wait_send()
 
 
-def copy_kernel(a, b, c, a_out, b_out, c_out, sem):
+def copy_kernel(a, b, c, a_out, b_out, c_out, held, sem_in, sem_out):
     pairs = ((a, a_out), (b, b_out), (c, c_out))
-    copies = [pltpu.make_async_copy(x, y, sem.at[i]) for i, (x, y) in enumerate(pairs)]
-    for copy in copies:
+    ins = [pltpu.make_async_copy(x, held.at[i], sem_in.at[i]) for i, (x, _) in enumerate(pairs)]
+    outs = [pltpu.make_async_copy(held.at[i], y, sem_out.at[i]) for i, (_, y) in enumerate(pairs)]
+    for copy in ins:
         copy.start()
-    for copy in copies:
+    for copy_in, copy_out in zip(ins, outs):
+        copy_in.wait()
+        copy_out.start()
+    for copy in outs:
         copy.wait()
 
 
@@ -545,7 +553,7 @@
         out_shape=(shape, shape, shape),
         in_specs=[pl.BlockSpec(memory_space=pltpu.HBM)] * 3,
         out_specs=[pl.BlockSpec(memory_space=pltpu.HBM)] * 3,
-        scratch_shapes=[dma((3,))],
+        scratch_shapes=[pltpu.VMEM((3, rows, cols, width), jnp.bfloat16), dma((3,)), dma((3,))],
         compiler_params=pltpu.CompilerParams(vmem_limit_bytes=60 << 20),
     )(*results)
 

time: 150 us -> 136 us (0.907)
  Pallas kernels: 149 us -> 135 us
    pallas_call x1, Pallas kernels: 13 us -> 1.74 us  [shards(): pl.pallas_call(copy_kernel, out_shape=(shape, shape, shape), in_specs=[pl...]
    pallas_call x1, Pallas kernels: 136 us -> 133 us  [shards(): pl.pallas_call(functools.partial(kernel, n_lat, n_lon, rows, cols, groups...]
where the time goes in v4:
time: 136 us
  Pallas kernels  135 us (99%)
    pallas_call x1, Pallas kernels, shards(): pl.pallas_call(functools.partial(kernel, n_lat, n_lon, rows, cols, groups...  133 us

profile of v4, /device:TPU:256, one launch (start us, length us, event | category | flops | bytes accessed | tf_op | source)
XLA Modules:
  0.0 135.6 jit_solution(3069069743128473222)
XLA Ops:
  0.6 133.2 %shard_map.76 = (bf16[8,16,512]{2,1,0:T(8,128)(2,1)}, bf16[8,16,512]{2,1,0:T(8,128)(2,1)}, bf16[8,16,512]{2,1,0:T(8,128)(2,1)}) custom-call(bf16[8,16,512]{2,1,0:T(8,128)(2,1)} %q_ref.1, bf16[8,16,512]{2,1,0:T(8,128)(2,1)} %k_ref.1, bf16[8,16,512]{2,1,0:T(8,128)(2,1)} %v_ref.1, bf16[8,16,512]{2,1,0:T(8,128)(2,1)} %g_ref.1, s32[2,256]{1,0:T(2,128)} %reach_hbm.1), custom_call_target="tpu_custom_call" | custom-call | tf_op jit(solution)/shard_map/pallas_call | solution.py:515
  133.8 1.7 %shard_map.77 = (bf16[8,16,512]{2,1,0:T(8,128)(2,1)}, bf16[8,16,512]{2,1,0:T(8,128)(2,1)}, bf16[8,16,512]{2,1,0:T(8,128)(2,1)}) custom-call(bf16[8,16,512]{2,1,0:T(8,128)(2,1)} %get-tuple-element.6.a, bf16[8,16,512]{2,1,0:T(8,128)(2,1)} %get-tuple-element.7.b, bf16[8,16,512]{2,1,0:T(8,128)(2,1)} %get-tuple-element.8.c), custom_call_target="tpu_custom_call" | custom-call | tf_op jit(solution)/shard_map/pallas_call | solution.py:551

commit v5 on v4

--- a/solution.py
+++ b/solution.py
@@ -380,9 +380,13 @@
         key, value = outer_part(g, 0), outer_part(g, 1)
         query_grad = jnp.zeros((own, LANES), jnp.float32)
         stats = stat_own[...]
-        for h in range(GROUP):
-            grad_h = grad * in_head_half[h]
-            logits = dot_nt(query * in_head_half[h], key) * to_log2 + bias[...]
+        for h in range(0, GROUP, 2):
+            grad_h = jnp.concatenate([grad * in_head_half[h], grad * in_head_half[h + 1]], axis=0)
+            query_h = jnp.concatenate(
+                [query * in_head_half[h], query * in_head_half[h + 1]], axis=0
+            )
+            logits = (dot_nt(query_h, key) * to_log2).reshape(2, own, outer) + bias[...][None]
+            logits = logits.reshape(2 * own, outer)
             top = jnp.max(logits, axis=1, keepdims=True)
             weight = jnp.exp2(logits - top)
             total = jnp.sum(weight, axis=1, keepdims=True)
@@ -391,15 +395,17 @@
             grad_dot = jnp.sum(grad_h.astype(jnp.float32) * attended, axis=1, keepdims=True)
             grad_probs = dot_nt(grad_h, value)
             grad_scores = (probs * (grad_probs - grad_dot)).astype(jnp.bfloat16)
-            query_grad += dot_nn(grad_scores, key) * in_head[h]
+            both = dot_nn(grad_scores, key)
+            query_grad += both[:own] * in_head[h] + both[own:] * in_head[h + 1]
             log_total = (top + jnp.log(total) * LOG2E) * (1.0 / to_log2)
-            head = g * GROUP + h
             for part, stat_value in enumerate((log_total, grad_dot)):
                 rest = -stat_value
                 for piece in range(3):
                     kept = rest.astype(jnp.bfloat16).astype(jnp.float32)
                     rest = rest - kept
-                    stats = jnp.where(lane == (3 * part + piece) * 16 + head, kept, stats)
+                    for i in range(2):
+                        at = lane == (3 * part + piece) * 16 + g * GROUP + h + i
+                        stats = jnp.where(at, kept[i * own : (i + 1) * own], stats)
         stat_own[...] = stats
         dq_ref[g] = (query_grad * scale).astype(jnp.bfloat16).reshape(rows, cols, LANES)
         out_copy(g, 0).start()
@@ -444,18 +450,24 @@
         grad_stat = jnp.concatenate([grad, outer_stat], axis=1)
         key_grad = jnp.zeros((own, LANES), jnp.float32)
         value_grad = jnp.zeros((own, LANES), jnp.float32)
-        for h in range(GROUP):
-            mine = lane % 16 == g * GROUP + h
-            in_log = jnp.where(mine & (lane < 48), 1.0, 0.0).astype(jnp.bfloat16)
-            in_dot = jnp.where(mine & (lane >= 48) & (lane < 96), 1.0, 0.0).astype(jnp.bfloat16)
-            in_log = jnp.broadcast_to(in_log, (own, LANES))
-            in_dot = jnp.broadcast_to(in_dot, (own, LANES))
-            key_h = jnp.concatenate([key * in_head_half[h], in_log], axis=1)
-            value_h = jnp.concatenate([value * in_head_half[h], in_dot], axis=1)
-            probs = jnp.exp2(dot_nt(key_h, query_stat) * to_log2 + bias[...])
-            value_grad += dot_nn(probs.astype(jnp.bfloat16), grad) * in_head[h]
+        for h in range(0, GROUP, 2):
+            keys, values = [], []
+            for i in range(2):
+                mine = lane % 16 == g * GROUP + h + i
+                in_log = jnp.where(mine & (lane < 48), 1.0, 0.0).astype(jnp.bfloat16)
+                in_dot = jnp.where(mine & (lane >= 48) & (lane < 96), 1.0, 0.0).astype(jnp.bfloat16)
+                in_log = jnp.broadcast_to(in_log, (own, LANES))
+                in_dot = jnp.broadcast_to(in_dot, (own, LANES))
+                keys.append(jnp.concatenate([key * in_head_half[h + i], in_log], axis=1))
+                values.append(jnp.concatenate([value * in_head_half[h + i], in_dot], axis=1))
+            key_h, value_h = jnp.concatenate(keys, axis=0), jnp.concatenate(values, axis=0)
+            logits = (dot_nt(key_h, query_stat) * to_log2).reshape(2, own, outer) + bias[...][None]
+            probs = jnp.exp2(logits.reshape(2 * own, outer))
+            both = dot_nn(probs.astype(jnp.bfloat16), grad)
+            value_grad += both[:own] * in_head[h] + both[own:] * in_head[h + 1]
             grad_scores = (probs * dot_nt(value_h, grad_stat)).astype(jnp.bfloat16)
-            key_grad += dot_nn(grad_scores, query) * in_head[h]
+            both = dot_nn(grad_scores, query)
+            key_grad += both[:own] * in_head[h] + both[own:] * in_head[h + 1]
         dk_ref[g] = (key_grad * scale).astype(jnp.bfloat16).reshape(rows, cols, LANES)
         out_copy(g, 1).start()
         dv_ref[g] = value_grad.astype(jnp.bfloat16).reshape(rows, cols, LANES)

time: 136 us -> 132 us (0.971)
  Pallas kernels: 135 us -> 131 us
    pallas_call x1, Pallas kernels: 133 us -> 129 us  [shards(): pl.pallas_call(functools.partial(kernel, n_lat, n_lon, rows, cols, groups...]
where the time goes in v5:
time: 132 us; the launch traced here: 131 us
  Pallas kernels  131 us (99%)
    pallas_call x1, Pallas kernels, shards(): pl.pallas_call(functools.partial(kernel, n_lat, n_lon, rows, cols, groups...  129 us

profile of v5, /device:TPU:256, one launch (start us, length us, event | category | flops | bytes accessed | tf_op | source)
XLA Modules:
  0.0 131.3 jit_solution(4294158230530986341)
XLA Ops:
  0.6 128.9 %shard_map.76 = (bf16[8,16,512]{2,1,0:T(8,128)(2,1)}, bf16[8,16,512]{2,1,0:T(8,128)(2,1)}, bf16[8,16,512]{2,1,0:T(8,128)(2,1)}) custom-call(bf16[8,16,512]{2,1,0:T(8,128)(2,1)} %q_ref.1, bf16[8,16,512]{2,1,0:T(8,128)(2,1)} %k_ref.1, bf16[8,16,512]{2,1,0:T(8,128)(2,1)} %v_ref.1, bf16[8,16,512]{2,1,0:T(8,128)(2,1)} %g_ref.1, s32[2,256]{1,0:T(2,128)} %reach_hbm.1), custom_call_target="tpu_custom_call" | custom-call | tf_op jit(solution)/shard_map/pallas_call | solution.py:527
  129.6 1.7 %shard_map.77 = (bf16[8,16,512]{2,1,0:T(8,128)(2,1)}, bf16[8,16,512]{2,1,0:T(8,128)(2,1)}, bf16[8,16,512]{2,1,0:T(8,128)(2,1)}) custom-call(bf16[8,16,512]{2,1,0:T(8,128)(2,1)} %get-tuple-element.6.a, bf16[8,16,512]{2,1,0:T(8,128)(2,1)} %get-tuple-element.7.b, bf16[8,16,512]{2,1,0:T(8,128)(2,1)} %get-tuple-element.8.c), custom_call_target="tpu_custom_call" | custom-call | tf_op jit(solution)/shard_map/pallas_call | solution.py:563
